TPU v7x, 512 devices: a whole 4x8x8 slice. The times are simulated.
512 devices in a mesh: row: 64 (over y_hi, x, z), col: 8 (over y_lo, core).
Axes of the slice: x: 4, y: 8 (y_hi: 2, y_lo: 4; y = y_hi * 4 + y_lo), z: 8, core: 2. Of those that a mesh axis runs over, the one named last changes fastest.
Arguments:
- features: bfloat16 [131072, 256], P(('row', 'col')), may hold values from -6 to 6
- weight: bfloat16 [256, 256], replicated, may hold values from -0.375 to 0.375
- weight_self: bfloat16 [256, 256], replicated, may hold values from -0.375 to 0.375
- tile_values: bfloat16 [64, 256, 128, 128], P('row', 'col'), may hold values from -0.125 to 0.125
- tile_rows: int32 [64, 256], P('row', 'col'), may hold values from 0 to 1
- tile_cols: int32 [64, 256], P('row', 'col'), may hold values from 0 to 47
- tile_count: int32 [64, 8], P('row', 'col'), may hold values from 1 to 32, as said below
- cotangent: bfloat16 [131072, 256], P(('row', 'col')), may hold values from -6 to 6
Outputs:
- activations: bfloat16 [131072, 256], P(('row', 'col'))
- feature_grad: bfloat16 [131072, 256], P(('row', 'col'))
- weight_grad: float32 [256, 256], replicated
- self_grad: float32 [256, 256], replicated
Inputs may be any that keep to these rules, and one draw needn't show every extreme that they name: Slots 0 to tile_count - 1 of a node block are live, the others are ignored; some node block has all 32 slots live.
All inputs are finite; a program needn't handle non-finite values.
Results may differ from a plain program's by a relative error of at most 0.0052.
Values may be sent and summed in bfloat16 or wider, within the bound.
A program may use at most 64 MiB of HBM per device.

v0:
```python
import math

import jax
import jax.numpy as jnp
from jax import lax
from jax.sharding import PartitionSpec as P


def with_halo(cells, sides, width):
    for axis, dim in sides:
        count = lax.axis_size(axis)
        head = lax.slice_in_dim(cells, 0, width, axis=dim)
        tail = lax.slice_in_dim(cells, cells.shape[dim] - width, cells.shape[dim], axis=dim)
        cells = jnp.concatenate(
            [
                lax.ppermute(tail, axis, [(i, (i + 1) % count) for i in range(count)]),
                cells,
                lax.ppermute(head, axis, [((i + 1) % count, i) for i in range(count)]),
            ],
            axis=dim,
        )
    return cells


def passed_along(value, axis, steps):
    count = lax.axis_size(axis)
    pairs = [(source, (source + steps) % count) for source in range(count)]
    return lax.ppermute(value, axis, pairs)


def shards(features, weight, weight_self, tile_values, tile_rows, tile_cols, tile_count, cotangent):
    tile_block = tile_values[0]
    slot_rows = tile_rows[0]
    slot_cols = tile_cols[0]
    live_count = tile_count[0, 0]
    slot_total = tile_block.shape[0]
    tile_side = tile_block.shape[-1]
    node_rows = features.shape[0]
    width = features.shape[1]
    per_block = node_rows // tile_side
    col_count = lax.axis_size("col")
    row_count = lax.axis_size("row")
    span = col_count * per_block
    group = lax.all_gather(features, "col", axis=0, tiled=True)
    window = with_halo(group, (("row", 0),), group.shape[0])
    window_tiles = window.reshape(-1, tile_side, width)
    row_ids = jnp.arange(per_block, dtype=jnp.int32)
    tiles_part = tile_block
    rows_part = slot_rows
    live_part = jnp.arange(slot_total, dtype=jnp.int32) < live_count
    feat_tiles = window_tiles[slot_cols]
    selector = ((rows_part[None, :] == row_ids[:, None]) & live_part[None, :]).astype(jnp.bfloat16)
    masked = tiles_part[None, :, :, :] * selector[:, :, None, None]
    summed = jnp.einsum("ktij,tjf->kif", masked, feat_tiles, preferred_element_type=jnp.float32)
    aggregated = summed.reshape(node_rows, width).astype(jnp.bfloat16)
    pre_act = jnp.dot(aggregated, weight, preferred_element_type=jnp.float32) + jnp.dot(
        features, weight_self, preferred_element_type=jnp.float32
    )
    activations = jax.nn.silu(pre_act).astype(jnp.bfloat16)
    sigma = jax.nn.sigmoid(pre_act)
    grad_pre = (cotangent.astype(jnp.float32) * sigma * (1.0 + pre_act * (1.0 - sigma))).astype(
        jnp.bfloat16
    )
    weight_part = jnp.einsum("nf,ng->fg", aggregated, grad_pre, preferred_element_type=jnp.float32)
    self_part = jnp.einsum("nf,ng->fg", features, grad_pre, preferred_element_type=jnp.float32)
    grad_aggregated = jnp.einsum(
        "ng,fg->nf", grad_pre, weight, preferred_element_type=jnp.float32
    ).astype(jnp.bfloat16)
    self_feature = jnp.einsum(
        "ng,fg->nf", grad_pre, weight_self, preferred_element_type=jnp.float32
    )
    grad_tiles = grad_aggregated.reshape(per_block, tile_side, width)
    spread_zero = jnp.zeros((3 * span, tile_side, width), jnp.float32)
    tiles_part = tile_block
    rows_part = slot_rows
    live_part = (jnp.arange(slot_total, dtype=jnp.int32) < live_count).astype(jnp.float32)
    picked = grad_tiles[rows_part]
    products = jnp.einsum("tij,tif->tjf", tiles_part, picked, preferred_element_type=jnp.float32)
    spread = spread_zero.at[slot_cols].add(products * live_part[:, None, None])
    spread = spread.reshape(3, col_count * node_rows, width)
    middle = spread[1]
    for offset in (1, -1):
        outgoing = spread[2] if offset == 1 else spread[0]
        middle = middle + passed_along(outgoing, "row", offset)
    own_share = lax.psum_scatter(middle, "col", scatter_dimension=0, tiled=True)
    feature_grad = (own_share + self_feature).astype(jnp.bfloat16)
    weight_total, self_total = lax.psum((weight_part, self_part), ("row", "col"))
    factor = 1.0 / math.sqrt(node_rows * col_count * row_count)
    return (activations, feature_grad, weight_total * factor, self_total * factor)


def solution(mesh):
    placed = (
        P(("row", "col"), None),
        P(),
        P(),
        P("row", "col", None, None),
        P("row", "col"),
        P("row", "col"),
        P("row", "col"),
        P(("row", "col"), None),
    )
    return jax.shard_map(
        shards,
        mesh=mesh,
        in_specs=placed,
        out_specs=(P(("row", "col"), None), P(("row", "col"), None), P(), P()),
        check_vma=False,
    )
```

profile of v0, /device:TPU:57, one launch (start us, length us, event | category | flops | bytes accessed | tf_op | source)
XLA Modules:
  0.0 519.9 jit_solution(5023080746673470452)
XLA Ops:
  7.2 0.0 copy-start
  7.2 0.0 all-gather.2.cloned.1.call-start
  7.2 0.7 all-gather.2.cloned.1.call-update
  7.9 0.0 all-reduce.3.cloned.1.call-start
  8.6 46.0 %all-gather.2.cloned.1.call-done = bf16[2048,256]{1,0:T(8,128)(2,1)} async-done(((bf16[256,256]{1,0:T(8,128)(2,1)}), bf16[2048,256]{1,0:T(8,128)(2,1)}) %all-gather.2.cloned.1.call-update) | async-done | bytes 1048592 | tf_op jit(solution)/shard_map/all_gather | solution.py:44
  54.6 7.7 %collective-permute-start.1 = (bf16[2048,256]{1,0:T(8,128)(2,1)}, bf16[2048,256]{1,0:T(8,128)(2,1)S(1)}, u32[]{:S(2)}, u32[]{:S(2)}) collective-permute-start(bf16[2048,256]{1,0:T(8,128)(2,1)} %all-gather.2.cloned.1.call-done), channel_id=1, source_target_pairs={{8,0},{16,8},{24,16},{32,24},{40,32},{48,40},{56,48},{64,56},{72,6... | collective-permute-start | bytes 3145736 | tf_op jit(solution)/shard_map/ppermute | solution.py:18
  62.3 1.9 collective-permute-start
  64.2 0.7 fusion.16
  64.9 0.7 fusion.17
  65.5 0.7 and_convert_fusion
  66.2 40.3 %collective-permute-done.1 = bf16[2048,256]{1,0:T(8,128)(2,1)S(1)} collective-permute-done((bf16[2048,256]{1,0:T(8,128)(2,1)}, bf16[2048,256]{1,0:T(8,128)(2,1)S(1)}, u32[]{:S(2)}, u32[]{:S(2)}) %collective-permute-start.1) | collective-permute-done | bytes 1048608 | tf_op jit(solution)/shard_map/ppermute | solution.py:18
  106.5 12.1 %collective-permute-done = bf16[2048,256]{1,0:T(8,128)(2,1)S(1)} collective-permute-done((bf16[2048,256]{1,0:T(8,128)(2,1)}, bf16[2048,256]{1,0:T(8,128)(2,1)S(1)}, u32[]{:S(2)}, u32[]{:S(2)}) %collective-permute-start) | collective-permute-done | bytes 1048608 | tf_op jit(solution)/shard_map/ppermute | solution.py:16
  118.6 1.6 pad_maximum_fusion
  120.3 2.0 gather_fusion
  122.3 2.7 fusion.9
  125.0 0.0 copy-start.5
  125.0 0.0 copy-done.2
  125.0 0.2 fusion.21
  125.2 0.0 copy-done
  125.2 0.0 copy-done.3
  125.2 0.0 copy-done.7
  125.3 0.9 multiply_convert_fusion
  126.2 0.2 convolution_convert_fusion
  126.4 0.0 copy-done.5
  126.4 0.0 copy-start.1
  126.4 0.7 gather_fusion.1
  127.1 0.5 copy-done.1
  127.7 2.9 multiply_bitcast_fusion
  130.6 5.6 %copy.15 = f32[32,128,256]{2,1,0:T(8,128)} copy(f32[32,128,256]{1,2,0:T(8,128)} %multiply_bitcast_fusion) | data formatting | bytes 8388608 | tf_op jit(solution)/shard_map/mul | solution.py:79
  136.2 3.4 broadcast_in_dim.2
  139.6 9.9 %scatter_fusion = f32[48,128,256]{2,1,0:T(8,128)} fusion(f32[48,128,256]{2,1,0:T(8,128)} %broadcast_in_dim.2, s32[32]{0:T(128)S(1)} %fusion.16, f32[32,128,256]{2,1,0:T(8,128)} %copy.15), kind=kCustom, calls=%fused_computation.2 | custom fusion | flops 1048576 | bytes 12583040 | tf_op jit(solution)/shard_map/scatter-add | solution.py:79
  149.5 5.6 %fusion.20 = (f32[16,128,256]{2,1,0:T(8,128)S(1)}, f32[16,128,256]{2,1,0:T(8,128)}, f32[16,128,256]{2,1,0:T(8,128)}) fusion(f32[48,128,256]{2,1,0:T(8,128)} %scatter_fusion), kind=kLoop, calls=%fused_computation.33 | loop fusion | bytes 12582912 | tf_op jit(solution)/shard_map/slice | solution.py:81
  155.1 1.9 collective-permute-start.3
  157.0 3.4 collective-permute-start.2
  160.4 0.0 copy-done.6
  160.4 0.9 fusion.23
  161.3 0.9 convolution_bitcast_fusion
  162.2 0.0 all-reduce.3.cloned.1.call-update
  162.3 0.0 reduce-scatter.2.cloned.1.call-start
  162.3 59.2 %collective-permute-done.3 = f32[2048,256]{1,0:T(8,128)} collective-permute-done((f32[2048,256]{1,0:T(8,128)}, f32[2048,256]{1,0:T(8,128)}, u32[]{:S(2)}, u32[]{:S(2)}) %collective-permute-start.3) | collective-permute-done | bytes 2097184 | tf_op jit(solution)/shard_map/ppermute | solution.py:28
  221.6 12.3 %collective-permute-done.2 = f32[2048,256]{1,0:T(8,128)} collective-permute-done((f32[2048,256]{1,0:T(8,128)}, f32[2048,256]{1,0:T(8,128)}, u32[]{:S(2)}, u32[]{:S(2)}) %collective-permute-start.2) | collective-permute-done | bytes 2097184 | tf_op jit(solution)/shard_map/ppermute | solution.py:28
  233.8 4.0 fusion
  237.8 0.0 reduce-scatter.2.cloned.1.call-update
  237.8 0.2 fusion.22
  238.1 228.6 %all-reduce.3.cloned.1.call-done = (f32[256,256]{1,0:T(8,128)}, f32[256,256]{1,0:T(8,128)}) async-done(((f32[256,256]{1,0:T(8,128)}, f32[256,256]{1,0:T(8,128)}), (f32[256,256]{1,0:T(8,128)}, f32[256,256]{1,0:T(8,128)})) %all-reduce.3.cloned.1.call-update) | async-done | bytes 524304 | tf_op jit(solution)/shard_map/psum | solution.py:87
  466.7 1.9 broadcast_multiply_fusion
  468.5 43.2 %reduce-scatter.2.cloned.1.call-done = f32[256,256]{1,0:T(8,128)} async-done(((f32[2048,256]{1,0:T(8,128)}), f32[256,256]{1,0:T(8,128)}) %reduce-scatter.2.cloned.1.call-update) | async-done | bytes 262160 | tf_op jit(solution)/shard_map/reduce_scatter | solution.py:85
  511.7 1.6 add_convert_fusion
  (10 shorter events, 0.0 us)
Async XLA Ops:
  7.2 118.1 %copy-start = (bf16[256,256]{1,0:T(8,128)(2,1)S(1)}, bf16[256,256]{1,0:T(8,128)(2,1)}, u32[]{:S(2)}) copy-start(bf16[256,256]{1,0:T(8,128)(2,1)} %param.10) | copy-start | bytes 393220
  7.2 47.4 %all-gather.2.cloned.1.call-start = ((), (), s32[]{:S(2)}) async-start(), calls=%async_computation.1 | async-start | bytes 1179648 | tf_op jit(solution)/shard_map/all_gather | solution.py:44
  7.9 458.7 %all-reduce.3.cloned.1.call-start = ((), (), s32[]{:S(2)}) async-start(), calls=%async_computation.3 | async-start | bytes 1048576 | tf_op jit(solution)/shard_map/psum | solution.py:87
  54.6 52.0 %collective-permute-start.1 = (bf16[2048,256]{1,0:T(8,128)(2,1)}, bf16[2048,256]{1,0:T(8,128)(2,1)S(1)}, u32[]{:S(2)}, u32[]{:S(2)}) collective-permute-start(bf16[2048,256]{1,0:T(8,128)(2,1)} %all-gather.2.cloned.1.call-done), channel_id=1, source_target_pairs={{8,0},{16,8},{24,16},{32,24},{40,32},{48,40},{56,48},{64,56},{72,6... | collective-permute-start | bytes 3145736 | tf_op jit(solution)/shard_map/ppermute | solution.py:18
  62.3 56.4 %collective-permute-start = (bf16[2048,256]{1,0:T(8,128)(2,1)}, bf16[2048,256]{1,0:T(8,128)(2,1)S(1)}, u32[]{:S(2)}, u32[]{:S(2)}) collective-permute-start(bf16[2048,256]{1,0:T(8,128)(2,1)} %all-gather.2.cloned.1.call-done), channel_id=1, source_target_pairs={{0,8},{8,16},{16,24},{24,32},{32,40},{40,48},{48,56},{56,64},{64,7... | collective-permute-start | bytes 3145736 | tf_op jit(solution)/shard_map/ppermute | solution.py:16
  122.3 2.7 copy-start.2
  122.3 2.9 copy-start.3
  122.3 2.9 copy-start.7
  125.0 1.4 copy-start.5
  126.4 1.2 copy-start.1
  149.5 10.9 %copy-start.6 = (bf16[2,128,256]{2,1,0:T(8,128)(2,1)S(1)}, bf16[2,128,256]{2,1,0:T(8,128)(2,1)}, u32[]{:S(2)}) copy-start(bf16[2,128,256]{2,1,0:T(8,128)(2,1)} %copy-done.5) | copy-start | bytes 393220
  149.5 11.8 %copy-start.4 = (bf16[256,256]{1,0:T(8,128)(2,1)S(1)}, bf16[256,256]{1,0:T(8,128)(2,1)}, u32[]{:S(2)}) copy-start(bf16[256,256]{1,0:T(8,128)(2,1)} %param.8) | copy-start | bytes 393220
  155.1 66.5 %collective-permute-start.3 = (f32[2048,256]{1,0:T(8,128)}, f32[2048,256]{1,0:T(8,128)}, u32[]{:S(2)}, u32[]{:S(2)}) collective-permute-start(f32[2048,256]{1,0:T(8,128)} %bitcast.16), channel_id=1, source_target_pairs={{0,504},{8,0},{16,8},{24,16},{32,24},{40,32},{48,40},{56,48},{64,5... | collective-permute-start | bytes 6291464 | tf_op jit(solution)/shard_map/ppermute | solution.py:28
  157.0 76.9 %collective-permute-start.2 = (f32[2048,256]{1,0:T(8,128)}, f32[2048,256]{1,0:T(8,128)}, u32[]{:S(2)}, u32[]{:S(2)}) collective-permute-start(f32[2048,256]{1,0:T(8,128)} %bitcast.15), channel_id=1, source_target_pairs={{0,8},{8,16},{16,24},{24,32},{32,40},{40,48},{48,56},{56,64},{64,7... | collective-permute-start | bytes 6291464 | tf_op jit(solution)/shard_map/ppermute | solution.py:28
  162.3 349.4 %reduce-scatter.2.cloned.1.call-start = ((), (), s32[]{:S(2)}) async-start(), calls=%async_computation.2 | async-start | bytes 2359296 | tf_op jit(solution)/shard_map/reduce_scatter | solution.py:85
Sparse Core Ops, SparseCore 0:
  10.1 44.4 all-gather.1
  162.4 304.2 all-reduce.2
  469.7 41.9 reduce-scatter.1
where the time goes:
time: 521 us; the launch traced here: 520 us
  waiting for transfers between devices  442 us (85%)
  other arithmetic  21 us (4%)
  local copies, waits for them, and re-layouts  17.9 us (3%)
  starting transfers between devices  15 us (3%)
  between operations  14.6 us (3%)
  matrix products  9.04 us (2%)
    psum x1, waiting for transfers between devices, shards(): lax.psum((weight_part, self_part), ('row', 'col'))  229 us
    ppermute x2, waiting for transfers between devices, passed_along(): return lax.ppermute(value, axis, pairs)  71.5 us
    all_gather x1, waiting for transfers between devices, shards(): group = lax.all_gather(features, 'col', axis=0, tiled=True)  46 us
    reduce_scatter x1, waiting for transfers between devices, shards(): own_share = lax.psum_scatter(middle, 'col', scatter_dimension=0, tiled=True)  43.2 us
    ppermute x1, waiting for transfers between devices, with_halo(): lax.ppermute(head, axis, [((i + 1) % count, i) for i in range(count)])  40.3 us
    ppermute x1, waiting for transfers between devices, with_halo(): lax.ppermute(tail, axis, [(i, (i + 1) % count) for i in range(count)])  12.1 us
  transfers between devices with their start and end apart: 7, of which 7 were waited for; matrix products, arithmetic and copies ran while one was open for 2% of the time, Pallas kernels for 0%

commit v1 on v0

--- a/solution.py
+++ b/solution.py
@@ -1,9 +1,119 @@
+import functools
 import math
 
 import jax
 import jax.numpy as jnp
 from jax import lax
+from jax.experimental import pallas as pl
+from jax.experimental.pallas import tpu as pltpu
 from jax.sharding import PartitionSpec as P
+
+MESH = pl.DeviceIdType.MESH
+
+
+def flip(index, stride):
+    bit = (index // stride) % 2
+    return index + stride - 2 * stride * bit, bit
+
+
+def allreduce_kernel(n_row, n_col, x_ref, o_ref, part, gath, rsend, rrecv, dsend, drecv, gsend, grecv):
+    row = lax.axis_index("row")
+    col = lax.axis_index("col")
+    col_bits = n_col.bit_length() - 1
+    row_bits = n_row.bit_length() - 1
+    partners = []
+    for k in range(col_bits):
+        partners.append((row, flip(col, 1 << k)[0]))
+    for k in range(row_bits):
+        partners.append((flip(row, 1 << k)[0], col))
+    barrier = pltpu.get_barrier_semaphore()
+    for device in partners:
+        pl.semaphore_signal(barrier, inc=1, device_id=device, device_id_type=MESH)
+    pl.semaphore_wait(barrier, len(partners))
+
+    rows = x_ref.shape[0]
+    src = x_ref
+    base = 0
+    size = rows
+    for k in range(col_bits):
+        other, bit = flip(col, 1 << k)
+        half = size // 2
+        keep = base + bit * half
+        give = base + (1 - bit) * half
+        copy = pltpu.make_async_remote_copy(
+            src_ref=src.at[pl.ds(pl.multiple_of(give, 8), half)],
+            dst_ref=part.at[k, pl.ds(0, half)],
+            send_sem=rsend.at[k],
+            recv_sem=rrecv.at[k],
+            device_id=(row, other),
+            device_id_type=MESH,
+        )
+        copy.start()
+        copy.wait()
+        mine = src[pl.ds(pl.multiple_of(keep, 8), half), :] + part[k, pl.ds(0, half), :]
+        gath[k, pl.ds(pl.multiple_of(keep, 8), half), :] = mine
+        src = gath.at[k]
+        base = keep
+        size = half
+    chunk = size
+    total = gath[col_bits - 1, pl.ds(pl.multiple_of(base, 8), chunk), :]
+    for k in range(row_bits):
+        other, _ = flip(row, 1 << k)
+        hold = o_ref.at[pl.ds(0, chunk)]
+        hold[...] = total
+        copy = pltpu.make_async_remote_copy(
+            src_ref=hold,
+            dst_ref=part.at[col_bits + k, pl.ds(0, chunk)],
+            send_sem=dsend.at[k],
+            recv_sem=drecv.at[k],
+            device_id=(other, col),
+            device_id_type=MESH,
+        )
+        copy.start()
+        copy.wait()
+        total = total + part[col_bits + k, pl.ds(0, chunk), :]
+    final = gath.at[col_bits]
+    final[pl.ds(pl.multiple_of(base, 8), chunk), :] = total
+    size = chunk
+    for k in reversed(range(col_bits)):
+        other, bit = flip(col, 1 << k)
+        start = base - bit * size
+        copy = pltpu.make_async_remote_copy(
+            src_ref=final.at[pl.ds(pl.multiple_of(base, 8), size)],
+            dst_ref=final.at[pl.ds(pl.multiple_of(base, 8), size)],
+            send_sem=gsend.at[k],
+            recv_sem=grecv.at[k],
+            device_id=(row, other),
+            device_id_type=MESH,
+        )
+        copy.start()
+        copy.wait()
+        base = start
+        size = size * 2
+    o_ref[...] = final[...]
+
+
+def all_reduce(stacked, n_row, n_col):
+    rows, width = stacked.shape
+    col_bits = n_col.bit_length() - 1
+    row_bits = n_row.bit_length() - 1
+    return pl.pallas_call(
+        functools.partial(allreduce_kernel, n_row, n_col),
+        out_shape=jax.ShapeDtypeStruct((rows, width), jnp.float32),
+        in_specs=[pl.BlockSpec(memory_space=pltpu.VMEM)],
+        out_specs=pl.BlockSpec(memory_space=pltpu.VMEM),
+        scratch_shapes=[
+            pltpu.VMEM((col_bits + row_bits, rows // 2, width), jnp.float32),
+            pltpu.VMEM((col_bits + 1, rows, width), jnp.float32),
+            pltpu.SemaphoreType.DMA((col_bits,)),
+            pltpu.SemaphoreType.DMA((col_bits,)),
+            pltpu.SemaphoreType.DMA((row_bits,)),
+            pltpu.SemaphoreType.DMA((row_bits,)),
+            pltpu.SemaphoreType.DMA((col_bits,)),
+            pltpu.SemaphoreType.DMA((col_bits,)),
+        ],
+        compiler_params=pltpu.CompilerParams(collective_id=0, has_side_effects=True),
+    )(stacked)
 
 
 def with_halo(cells, sides, width):
@@ -84,7 +194,10 @@
         middle = middle + passed_along(outgoing, "row", offset)
     own_share = lax.psum_scatter(middle, "col", scatter_dimension=0, tiled=True)
     feature_grad = (own_share + self_feature).astype(jnp.bfloat16)
-    weight_total, self_total = lax.psum((weight_part, self_part), ("row", "col"))
+    summed_parts = all_reduce(
+        jnp.concatenate([weight_part, self_part], axis=0), row_count, col_count
+    )
+    weight_total, self_total = summed_parts[:width], summed_parts[width:]
     factor = 1.0 / math.sqrt(node_rows * col_count * row_count)
     return (activations, feature_grad, weight_total * factor, self_total * factor)
 

time: 521 us -> 307 us (0.59)
  waiting for transfers between devices: 442 us -> 171 us
  Pallas kernels: 0 us -> 56.2 us
    psum x1 -> x0, waiting for transfers between devices: 229 us -> none  [shards(): lax.psum((weight_part, self_part), ('row', 'col'))]
    pallas_call x0 -> x1, Pallas kernels: none -> 56.2 us  [all_reduce(): pl.pallas_call(functools.partial(allreduce_kernel, n_row, n_col), out_sha...]
    reduce_scatter x1, waiting for transfers between devices: 43.2 us -> 0.01 us  [shards(): own_share = lax.psum_scatter(middle, 'col', scatter_dimension=0, tiled=True)]
  transfers between devices with their start and end apart: 7 -> 6, of which waited for: 7 -> 5; matrix products, arithmetic and copies ran while one was open for 2% -> 2% of each run, Pallas kernels for 0% -> 19%
where the time goes in v1:
time: 307 us; the launch traced here: 302 us
  waiting for transfers between devices  171 us (56%)
  Pallas kernels  56.2 us (18%)
  other arithmetic  19.9 us (6%)
  local copies, waits for them, and re-layouts  16.7 us (5%)
  starting transfers between devices  15 us (5%)
  between operations  14.9 us (5%)
  matrix products  7.61 us (2%)
    ppermute x2, waiting for transfers between devices, passed_along(): return lax.ppermute(value, axis, pairs)  72.2 us
    pallas_call x1, Pallas kernels, all_reduce(): pl.pallas_call(functools.partial(allreduce_kernel, n_row, n_col), out_sha...  56.2 us
    all_gather x1, waiting for transfers between devices, shards(): group = lax.all_gather(features, 'col', axis=0, tiled=True)  46 us
    ppermute x1, waiting for transfers between devices, with_halo(): lax.ppermute(head, axis, [((i + 1) % count, i) for i in range(count)])  40.3 us
    ppermute x1, waiting for transfers between devices, with_halo(): lax.ppermute(tail, axis, [(i, (i + 1) % count) for i in range(count)])  12.1 us
    scatter-add x1, other arithmetic, shards(): spread = spread_zero.at[slot_cols].add(products * live_part[:, None, None])  10.1 us
    ppermute x1, starting transfers between devices, with_halo(): lax.ppermute(head, axis, [((i + 1) % count, i) for i in range(count)])  7.69 us
  transfers between devices with their start and end apart: 6, of which 5 were waited for; matrix products, arithmetic and copies ran while one was open for 2% of the time, Pallas kernels for 19%

profile of v1, /device:TPU:57, one launch (start us, length us, event | category | flops | bytes accessed | tf_op | source)
XLA Modules:
  0.0 301.6 jit_solution(14602053346739756531)
XLA Ops:
  7.2 0.0 copy-start
  7.2 0.0 all-gather.2.cloned.1.call-start
  7.2 0.7 all-gather.2.cloned.1.call-update
  7.9 0.0 reduce-scatter.2.cloned.1.call-start
  8.6 46.0 %all-gather.2.cloned.1.call-done = bf16[2048,256]{1,0:T(8,128)(2,1)} async-done(((bf16[256,256]{1,0:T(8,128)(2,1)}), bf16[2048,256]{1,0:T(8,128)(2,1)}) %all-gather.2.cloned.1.call-update) | async-done | bytes 1048592 | tf_op jit(solution)/shard_map/all_gather | solution.py:154
  54.6 7.7 %collective-permute-start.1 = (bf16[2048,256]{1,0:T(8,128)(2,1)}, bf16[2048,256]{1,0:T(8,128)(2,1)S(1)}, u32[]{:S(2)}, u32[]{:S(2)}) collective-permute-start(bf16[2048,256]{1,0:T(8,128)(2,1)} %all-gather.2.cloned.1.call-done), channel_id=1, source_target_pairs={{8,0},{16,8},{24,16},{32,24},{40,32},{48,40},{56,48},{64,56},{72,6... | collective-permute-start | bytes 3145736 | tf_op jit(solution)/shard_map/ppermute | solution.py:128
  62.3 1.9 collective-permute-start
  64.2 0.7 fusion.16
  64.9 0.7 fusion.17
  65.6 0.7 and_convert_fusion
  66.2 40.3 %collective-permute-done.1 = bf16[2048,256]{1,0:T(8,128)(2,1)S(1)} collective-permute-done((bf16[2048,256]{1,0:T(8,128)(2,1)}, bf16[2048,256]{1,0:T(8,128)(2,1)S(1)}, u32[]{:S(2)}, u32[]{:S(2)}) %collective-permute-start.1) | collective-permute-done | bytes 1048608 | tf_op jit(solution)/shard_map/ppermute | solution.py:128
  106.5 12.1 %collective-permute-done = bf16[2048,256]{1,0:T(8,128)(2,1)S(1)} collective-permute-done((bf16[2048,256]{1,0:T(8,128)(2,1)}, bf16[2048,256]{1,0:T(8,128)(2,1)S(1)}, u32[]{:S(2)}, u32[]{:S(2)}) %collective-permute-start) | collective-permute-done | bytes 1048608 | tf_op jit(solution)/shard_map/ppermute | solution.py:126
  118.6 1.6 pad_maximum_fusion
  120.3 2.0 gather_fusion
  122.3 0.0 copy-start.2
  122.3 2.7 fusion.9
  125.0 0.0 copy-start.5
  125.0 0.0 copy-done.2
  125.0 0.2 fusion.21
  125.2 0.0 copy-done
  125.2 0.0 copy-done.3
  125.2 0.0 copy-done.7
  125.2 0.9 multiply_convert_fusion
  126.2 0.2 convolution_convert_fusion
  126.4 0.0 copy-done.5
  126.4 0.0 copy-start.1
  126.4 0.7 gather_fusion.1
  127.1 0.5 copy-done.1
  127.6 2.9 multiply_bitcast_fusion
  130.6 5.6 %copy.14 = f32[32,128,256]{2,1,0:T(8,128)} copy(f32[32,128,256]{1,2,0:T(8,128)} %multiply_bitcast_fusion) | data formatting | bytes 8388608 | tf_op jit(solution)/shard_map/mul | solution.py:189
  136.1 3.4 %broadcast_in_dim.2 = f32[48,128,256]{2,1,0:T(8,128)} broadcast(f32[]{:T(128)} %constant.3.clone.1), dimensions={} | broadcast | bytes 6291460 | tf_op jit(solution)/shard_map/broadcast_in_dim | solution.py:183
  139.6 10.1 %scatter_fusion = f32[48,128,256]{2,1,0:T(8,128)} fusion(f32[48,128,256]{2,1,0:T(8,128)} %broadcast_in_dim.2, s32[32]{0:T(128)S(1)} %fusion.16, f32[32,128,256]{2,1,0:T(8,128)} %copy.14), kind=kCustom, calls=%fused_computation.2 | custom fusion | flops 1048576 | bytes 12583040 | tf_op jit(solution)/shard_map/scatter-add | solution.py:189
  149.7 3.6 %fusion.20 = (f32[16,128,256]{2,1,0:T(8,128)S(1)}, f32[16,128,256]{2,1,0:T(8,128)S(1)}, f32[16,128,256]{2,1,0:T(8,128)S(1)}) fusion(f32[48,128,256]{2,1,0:T(8,128)} %scatter_fusion), kind=kLoop, calls=%fused_computation.34 | loop fusion | bytes 12582912 | tf_op jit(solution)/shard_map/slice | solution.py:191
  153.2 1.9 collective-permute-start.3
  155.2 3.4 %collective-permute-start.2 = (f32[2048,256]{1,0:T(8,128)S(1)}, f32[2048,256]{1,0:T(8,128)S(1)}, u32[]{:S(2)}, u32[]{:S(2)}) collective-permute-start(f32[2048,256]{1,0:T(8,128)S(1)} %bitcast.55), channel_id=1, source_target_pairs={{0,8},{8,16},{16,24},{24,32},{32,40},{40,48},{48,56},{56,64},{64,7... | collective-permute-start | bytes 6291464 | tf_op jit(solution)/shard_map/ppermute | solution.py:138
  158.5 60.0 %collective-permute-done.3 = f32[2048,256]{1,0:T(8,128)S(1)} collective-permute-done((f32[2048,256]{1,0:T(8,128)S(1)}, f32[2048,256]{1,0:T(8,128)S(1)}, u32[]{:S(2)}, u32[]{:S(2)}) %collective-permute-start.3) | collective-permute-done | bytes 2097184 | tf_op jit(solution)/shard_map/ppermute | solution.py:138
  218.6 12.2 %collective-permute-done.2 = f32[2048,256]{1,0:T(8,128)S(1)} collective-permute-done((f32[2048,256]{1,0:T(8,128)S(1)}, f32[2048,256]{1,0:T(8,128)S(1)}, u32[]{:S(2)}, u32[]{:S(2)}) %collective-permute-start.2) | collective-permute-done | bytes 2097184 | tf_op jit(solution)/shard_map/ppermute | solution.py:138
  230.8 1.9 fusion
  232.7 0.0 reduce-scatter.2.cloned.1.call-update
  232.7 0.9 copy-done.4
  233.6 0.2 convolution_bitcast_fusion
  233.8 0.0 copy-done.6
  233.8 0.2 fusion.23
  234.0 0.8 pad_maximum_fusion.1.x_ref
  234.9 56.2 %shard_map.111 = f32[512,256]{1,0:T(8,128)} custom-call(f32[512,256]{1,0:T(8,128)} %pad_maximum_fusion.1.x_ref), custom_call_target="tpu_custom_call" | custom-call | tf_op jit(solution)/shard_map/pallas_call | solution.py:100
  291.1 0.2 fusion.22
  291.3 1.9 slice_multiply_fusion
  293.2 1.6 add_convert_fusion
  (9 shorter events, 0.0 us)
Async XLA Ops:
  7.2 118.0 %copy-start = (bf16[256,256]{1,0:T(8,128)(2,1)S(1)}, bf16[256,256]{1,0:T(8,128)(2,1)}, u32[]{:S(2)}) copy-start(bf16[256,256]{1,0:T(8,128)(2,1)} %param.10) | copy-start | bytes 393220
  7.2 47.4 %all-gather.2.cloned.1.call-start = ((), (), s32[]{:S(2)}) async-start(), calls=%async_computation.1 | async-start | bytes 1179648 | tf_op jit(solution)/shard_map/all_gather | solution.py:154
  7.9 285.2 %reduce-scatter.2.cloned.1.call-start = ((), (), s32[]{:S(2)}) async-start(), calls=%async_computation.2 | async-start | bytes 2359296 | tf_op jit(solution)/shard_map/reduce_scatter | solution.py:195
  54.6 52.0 %collective-permute-start.1 = (bf16[2048,256]{1,0:T(8,128)(2,1)}, bf16[2048,256]{1,0:T(8,128)(2,1)S(1)}, u32[]{:S(2)}, u32[]{:S(2)}) collective-permute-start(bf16[2048,256]{1,0:T(8,128)(2,1)} %all-gather.2.cloned.1.call-done), channel_id=1, source_target_pairs={{8,0},{16,8},{24,16},{32,24},{40,32},{48,40},{56,48},{64,56},{72,6... | collective-permute-start | bytes 3145736 | tf_op jit(solution)/shard_map/ppermute | solution.py:128
  62.3 56.4 %collective-permute-start = (bf16[2048,256]{1,0:T(8,128)(2,1)}, bf16[2048,256]{1,0:T(8,128)(2,1)S(1)}, u32[]{:S(2)}, u32[]{:S(2)}) collective-permute-start(bf16[2048,256]{1,0:T(8,128)(2,1)} %all-gather.2.cloned.1.call-done), channel_id=1, source_target_pairs={{0,8},{8,16},{16,24},{24,32},{32,40},{40,48},{48,56},{56,64},{64,7... | collective-permute-start | bytes 3145736 | tf_op jit(solution)/shard_map/ppermute | solution.py:126
  122.3 2.7 copy-start.2
  122.3 2.9 copy-start.3
  122.3 2.9 copy-start.7
  125.0 1.4 copy-start.5
  126.4 1.2 copy-start.1
  153.2 65.3 %collective-permute-start.3 = (f32[2048,256]{1,0:T(8,128)S(1)}, f32[2048,256]{1,0:T(8,128)S(1)}, u32[]{:S(2)}, u32[]{:S(2)}) collective-permute-start(f32[2048,256]{1,0:T(8,128)S(1)} %bitcast.56), channel_id=1, source_target_pairs={{0,504},{8,0},{16,8},{24,16},{32,24},{40,32},{48,40},{56,48},{64,5... | collective-permute-start | bytes 6291464 | tf_op jit(solution)/shard_map/ppermute | solution.py:138
  155.2 75.6 %collective-permute-start.2 = (f32[2048,256]{1,0:T(8,128)S(1)}, f32[2048,256]{1,0:T(8,128)S(1)}, u32[]{:S(2)}, u32[]{:S(2)}) collective-permute-start(f32[2048,256]{1,0:T(8,128)S(1)} %bitcast.55), channel_id=1, source_target_pairs={{0,8},{8,16},{16,24},{24,32},{32,40},{40,48},{48,56},{56,64},{64,7... | collective-permute-start | bytes 6291464 | tf_op jit(solution)/shard_map/ppermute | solution.py:138
  232.6 0.9 copy-start.4
  232.6 1.1 copy-start.6
Sparse Core Ops, SparseCore 0:
  10.1 44.4 all-gather.1
  232.8 45.2 reduce-scatter.1

commit v2 on v1

--- a/solution.py
+++ b/solution.py
@@ -91,6 +91,90 @@
         base = start
         size = size * 2
     o_ref[...] = final[...]
+
+
+def ring_position(col, n):
+    core = col % 2
+    y = col // 2
+    return y + core * (n - 1 - 2 * y)
+
+
+def ring_col(p, n):
+    q = p // (n // 2)
+    y = p + q * (n - 1 - 2 * p)
+    return 2 * y + q
+
+
+def gather_kernel(n_row, n_col, x_ref, w_ref, ring_send, ring_recv, up_send, up_recv, down_send, down_recv, local_sem):
+    row = lax.axis_index("row")
+    col = lax.axis_index("col")
+    p = ring_position(col, n_col)
+    succ = ring_col((p + 1) % n_col, n_col)
+    pred = ring_col((p + n_col - 1) % n_col, n_col)
+    up = (row + 1) % n_row
+    down = (row + n_row - 1) % n_row
+    barrier = pltpu.get_barrier_semaphore()
+    for device in ((row, succ), (row, pred), (up, col), (down, col)):
+        pl.semaphore_signal(barrier, inc=1, device_id=device, device_id_type=MESH)
+    pl.semaphore_wait(barrier, 4)
+    local = pltpu.make_async_copy(x_ref, w_ref.at[1, col], local_sem.at[0])
+    local.start()
+    halos = []
+
+    def halo(src, block, step):
+        for target, slot, send, recv in ((up, 0, up_send, up_recv), (down, 2, down_send, down_recv)):
+            copy = pltpu.make_async_remote_copy(
+                src_ref=src,
+                dst_ref=w_ref.at[slot, block],
+                send_sem=send.at[step],
+                recv_sem=recv.at[step],
+                device_id=(target, col),
+                device_id_type=MESH,
+            )
+            copy.start()
+            halos.append(copy)
+
+    halo(x_ref, col, 0)
+    src = x_ref
+    sent = col
+    for step in range(1, n_col):
+        got = ring_col((p - step + n_col) % n_col, n_col)
+        copy = pltpu.make_async_remote_copy(
+            src_ref=src,
+            dst_ref=w_ref.at[1, sent],
+            send_sem=ring_send.at[step - 1],
+            recv_sem=ring_recv.at[step - 1],
+            device_id=(row, succ),
+            device_id_type=MESH,
+        )
+        copy.start()
+        copy.wait()
+        src = w_ref.at[1, got]
+        sent = got
+        halo(src, got, step)
+    for copy in halos:
+        copy.wait()
+    local.wait()
+
+
+def gather_window(block, n_row, n_col):
+    rows, width = block.shape
+    return pl.pallas_call(
+        functools.partial(gather_kernel, n_row, n_col),
+        out_shape=jax.ShapeDtypeStruct((3, n_col, rows, width), block.dtype),
+        in_specs=[pl.BlockSpec(memory_space=pltpu.VMEM)],
+        out_specs=pl.BlockSpec(memory_space=pltpu.VMEM),
+        scratch_shapes=[
+            pltpu.SemaphoreType.DMA((n_col - 1,)),
+            pltpu.SemaphoreType.DMA((n_col - 1,)),
+            pltpu.SemaphoreType.DMA((n_col,)),
+            pltpu.SemaphoreType.DMA((n_col,)),
+            pltpu.SemaphoreType.DMA((n_col,)),
+            pltpu.SemaphoreType.DMA((n_col,)),
+            pltpu.SemaphoreType.DMA((1,)),
+        ],
+        compiler_params=pltpu.CompilerParams(collective_id=1, has_side_effects=True),
+    )(block)
 
 
 def all_reduce(stacked, n_row, n_col):
@@ -151,8 +235,7 @@
     col_count = lax.axis_size("col")
     row_count = lax.axis_size("row")
     span = col_count * per_block
-    group = lax.all_gather(features, "col", axis=0, tiled=True)
-    window = with_halo(group, (("row", 0),), group.shape[0])
+    window = gather_window(features, row_count, col_count)
     window_tiles = window.reshape(-1, tile_side, width)
     row_ids = jnp.arange(per_block, dtype=jnp.int32)
     tiles_part = tile_block

time: 307 us -> 298 us (0.971)
  waiting for transfers between devices: 171 us -> 97 us
  Pallas kernels: 56.2 us -> 127 us
  other arithmetic: 19.9 us -> 16.1 us
    pallas_call x0 -> x1, Pallas kernels: none -> 74.2 us  [gather_window(): pl.pallas_call(functools.partial(gather_kernel, n_row, n_col), out_shape=...]
    ppermute x2 -> x0, waiting for transfers between devices: 52.4 us -> none  [the longest x1 40.3 us: with_halo(): lax.ppermute(head, axis, [((i + 1) % count, i) for i in range(count)])]
    all_gather x1 -> x0, waiting for transfers between devices: 46 us -> none  [shards(): group = lax.all_gather(features, 'col', axis=0, tiled=True)]
    ppermute x2, waiting for transfers between devices: 72.2 us -> 97 us  [passed_along(): return lax.ppermute(value, axis, pairs)]
    ppermute x2 -> x0, starting transfers between devices: 9.61 us -> none  [the longest x1 7.69 us: with_halo(): lax.ppermute(head, axis, [((i + 1) % count, i) for i in range(count)])]
    ppermute x2, starting transfers between devices: 5.28 us -> 14.1 us  [passed_along(): return lax.ppermute(value, axis, pairs)]
    pallas_call x1, Pallas kernels: 56.2 us -> 52.7 us  [all_reduce(): pl.pallas_call(functools.partial(allreduce_kernel, n_row, n_col), out_sha...]
  transfers between devices with their start and end apart: 6 -> 3, of which waited for: 5 -> 2; matrix products, arithmetic and copies ran while one was open for 2% -> 1% of each run, Pallas kernels for 19% -> 18%
where the time goes in v2:
time: 298 us; the launch traced here: 292 us
  Pallas kernels  127 us (43%)
  waiting for transfers between devices  97 us (33%)
  local copies, waits for them, and re-layouts  17.5 us (6%)
  other arithmetic  16.1 us (5%)
  between operations  14.9 us (5%)
  starting transfers between devices  14.2 us (5%)
  matrix products  5.64 us (2%)
    ppermute x2, waiting for transfers between devices, passed_along(): return lax.ppermute(value, axis, pairs)  97 us
    pallas_call x1, Pallas kernels, gather_window(): pl.pallas_call(functools.partial(gather_kernel, n_row, n_col), out_shape=...  74.2 us
    pallas_call x1, Pallas kernels, all_reduce(): pl.pallas_call(functools.partial(allreduce_kernel, n_row, n_col), out_sha...  52.7 us
    ppermute x2, starting transfers between devices, passed_along(): return lax.ppermute(value, axis, pairs)  14.1 us
    scatter-add x1, other arithmetic, shards(): spread = spread_zero.at[slot_cols].add(products * live_part[:, None, None])  9.85 us
  transfers between devices with their start and end apart: 3, of which 2 were waited for; matrix products, arithmetic and copies ran while one was open for 1% of the time, Pallas kernels for 18%

profile of v2, /device:TPU:57, one launch (start us, length us, event | category | flops | bytes accessed | tf_op | source)
XLA Modules:
  0.0 292.2 jit_solution(6134065353478175010)
XLA Ops:
  7.2 0.0 copy-start
  7.2 0.0 copy-start.8
  7.2 0.0 copy-start.9
  7.2 0.0 reduce-scatter.2.cloned.1.call-start
  7.2 74.2 %shard_map.111 = bf16[3,8,256,256]{3,2,1,0:T(8,128)(2,1)} custom-call(bf16[256,256]{1,0:T(8,128)(2,1)} %x_ref.1), custom_call_target="tpu_custom_call" | custom-call | tf_op jit(solution)/shard_map/pallas_call | solution.py:162
  81.5 0.0 copy-done.8
  82.2 0.0 copy-done.9
  82.2 0.0 copy-start.1
  82.2 2.7 gather_fusion
  84.9 0.0 copy-done.1
  84.9 0.0 copy-start.2
  84.9 0.0 copy-start.3
  84.9 0.0 copy-start.7
  84.9 0.7 fusion.9
  85.7 0.0 copy-start.5
  85.7 0.6 copy-done.5
  86.4 0.0 copy-done.2
  86.4 0.2 fusion.21
  86.5 0.0 copy-done
  86.6 0.0 copy-done.3
  86.6 0.0 copy-done.7
  86.6 0.9 multiply_convert_fusion
  87.5 0.2 convolution_convert_fusion
  87.8 0.7 gather_fusion.1
  88.4 2.9 multiply_bitcast_fusion
  91.3 5.6 %copy.14 = f32[32,128,256]{2,1,0:T(8,128)} copy(f32[32,128,256]{1,2,0:T(8,128)} %multiply_bitcast_fusion) | data formatting | bytes 8388608 | tf_op jit(solution)/shard_map/mul | solution.py:272
  96.9 3.4 %broadcast_in_dim.2 = f32[48,128,256]{2,1,0:T(8,128)} broadcast(f32[]{:T(128)} %constant.3.clone.1), dimensions={} | broadcast | bytes 6291460 | tf_op jit(solution)/shard_map/broadcast_in_dim | solution.py:266
  100.3 9.8 %scatter_fusion = f32[48,128,256]{2,1,0:T(8,128)} fusion(f32[48,128,256]{2,1,0:T(8,128)} %broadcast_in_dim.2, s32[32]{0:T(128)S(1)} %fusion.16, f32[32,128,256]{2,1,0:T(8,128)} %copy.14), kind=kCustom, calls=%fused_computation.2 | custom fusion | flops 1048576 | bytes 12583040 | tf_op jit(solution)/shard_map/scatter-add | solution.py:272
  110.2 3.6 %fusion.20 = (f32[16,128,256]{2,1,0:T(8,128)S(1)}, f32[16,128,256]{2,1,0:T(8,128)S(1)}, f32[16,128,256]{2,1,0:T(8,128)S(1)}) fusion(f32[48,128,256]{2,1,0:T(8,128)} %scatter_fusion), kind=kLoop, calls=%fused_computation.33 | loop fusion | bytes 12582912 | tf_op jit(solution)/shard_map/slice | solution.py:274
  113.8 12.2 %collective-permute-start.1 = (f32[2048,256]{1,0:T(8,128)S(1)}, f32[2048,256]{1,0:T(8,128)S(1)}, u32[]{:S(2)}, u32[]{:S(2)}) collective-permute-start(f32[2048,256]{1,0:T(8,128)S(1)} %bitcast.55), channel_id=1, source_target_pairs={{0,504},{8,0},{16,8},{24,16},{32,24},{40,32},{48,40},{56,48},{64,5... | collective-permute-start | bytes 6291464 | tf_op jit(solution)/shard_map/ppermute | solution.py:222
  126.0 1.9 collective-permute-start
  127.9 84.9 %collective-permute-done.1 = f32[2048,256]{1,0:T(8,128)S(1)} collective-permute-done((f32[2048,256]{1,0:T(8,128)S(1)}, f32[2048,256]{1,0:T(8,128)S(1)}, u32[]{:S(2)}, u32[]{:S(2)}) %collective-permute-start.1) | collective-permute-done | bytes 2097184 | tf_op jit(solution)/shard_map/ppermute | solution.py:222
  212.8 12.1 %collective-permute-done = f32[2048,256]{1,0:T(8,128)S(1)} collective-permute-done((f32[2048,256]{1,0:T(8,128)S(1)}, f32[2048,256]{1,0:T(8,128)S(1)}, u32[]{:S(2)}, u32[]{:S(2)}) %collective-permute-start) | collective-permute-done | bytes 2097184 | tf_op jit(solution)/shard_map/ppermute | solution.py:222
  224.9 1.9 fusion
  226.8 0.0 copy-start.4
  226.8 0.0 copy-start.6
  226.8 0.0 reduce-scatter.2.cloned.1.call-update
  226.8 0.9 copy-done.4
  227.7 0.2 convolution_bitcast_fusion
  227.9 0.0 copy-done.6
  227.9 0.2 fusion.23
  228.2 0.8 pad_maximum_fusion.x_ref
  229.0 52.7 %shard_map.112 = f32[512,256]{1,0:T(8,128)} custom-call(f32[512,256]{1,0:T(8,128)} %pad_maximum_fusion.x_ref), custom_call_target="tpu_custom_call" | custom-call | tf_op jit(solution)/shard_map/pallas_call | solution.py:184
  281.7 0.2 fusion.22
  281.9 1.9 slice_multiply_fusion
  283.7 0.0 reduce-scatter.2.cloned.1.call-done
  283.7 1.6 add_convert_fusion
  (6 shorter events, 0.0 us)
Async XLA Ops:
  7.2 79.4 %copy-start = (bf16[256,256]{1,0:T(8,128)(2,1)S(1)}, bf16[256,256]{1,0:T(8,128)(2,1)}, u32[]{:S(2)}) copy-start(bf16[256,256]{1,0:T(8,128)(2,1)} %param.10) | copy-start | bytes 393220
  7.2 74.3 %copy-start.8 = (s32[1,32]{1,0:T(1,128)S(1)}, s32[1,32]{1,0:T(1,128)}, u32[]{:S(2)}) copy-start(s32[1,32]{1,0:T(1,128)} %param.13) | copy-start | bytes 388
  7.2 75.0 %copy-start.9 = (s32[1,32]{1,0:T(1,128)S(1)}, s32[1,32]{1,0:T(1,128)}, u32[]{:S(2)}) copy-start(s32[1,32]{1,0:T(1,128)} %param.12) | copy-start | bytes 388
  7.2 276.5 %reduce-scatter.2.cloned.1.call-start = ((), (), s32[]{:S(2)}) async-start(), calls=%async_computation.1 | async-start | bytes 2359296 | tf_op jit(solution)/shard_map/reduce_scatter | solution.py:278
  82.2 2.7 copy-start.1
  84.9 1.4 copy-start.2
  84.9 1.6 copy-start.3
  84.9 1.6 copy-start.7
  85.7 0.7 copy-start.5
  113.8 99.1 %collective-permute-start.1 = (f32[2048,256]{1,0:T(8,128)S(1)}, f32[2048,256]{1,0:T(8,128)S(1)}, u32[]{:S(2)}, u32[]{:S(2)}) collective-permute-start(f32[2048,256]{1,0:T(8,128)S(1)} %bitcast.55), channel_id=1, source_target_pairs={{0,504},{8,0},{16,8},{24,16},{32,24},{40,32},{48,40},{56,48},{64,5... | collective-permute-start | bytes 6291464 | tf_op jit(solution)/shard_map/ppermute | solution.py:222
  126.0 99.0 %collective-permute-start = (f32[2048,256]{1,0:T(8,128)S(1)}, f32[2048,256]{1,0:T(8,128)S(1)}, u32[]{:S(2)}, u32[]{:S(2)}) collective-permute-start(f32[2048,256]{1,0:T(8,128)S(1)} %bitcast.54), channel_id=1, source_target_pairs={{0,8},{8,16},{16,24},{24,32},{32,40},{40,48},{48,56},{56,64},{64,7... | collective-permute-start | bytes 6291464 | tf_op jit(solution)/shard_map/ppermute | solution.py:222
  226.8 0.9 copy-start.4
  226.8 1.1 copy-start.6
Sparse Core Ops, SparseCore 0:
  226.9 39.2 reduce-scatter.1

commit v3 on v2

--- a/solution.py
+++ b/solution.py
@@ -175,6 +175,93 @@
         ],
         compiler_params=pltpu.CompilerParams(collective_id=1, has_side_effects=True),
     )(block)
+
+
+def spread_kernel(n_row, n_col, mid_ref, up_ref, down_ref, o_ref, from_down, from_up, ring_in, ring_out,
+                  up_send, down_send, from_down_sem, from_up_sem, ring_send, ring_recv):
+    row = lax.axis_index("row")
+    col = lax.axis_index("col")
+    p = ring_position(col, n_col)
+    succ = ring_col((p + 1) % n_col, n_col)
+    pred = ring_col((p + n_col - 1) % n_col, n_col)
+    up = (row + 1) % n_row
+    down = (row + n_row - 1) % n_row
+    barrier = pltpu.get_barrier_semaphore()
+    for device in ((row, succ), (row, pred), (up, col), (down, col)):
+        pl.semaphore_signal(barrier, inc=1, device_id=device, device_id_type=MESH)
+    pl.semaphore_wait(barrier, 4)
+    halos = []
+    for step in range(1, n_col + 1):
+        block = ring_col((p - step + 2 * n_col) % n_col, n_col)
+        pair = []
+        for src, dst, target, send, recv in (
+            (up_ref, from_down, up, up_send, from_down_sem),
+            (down_ref, from_up, down, down_send, from_up_sem),
+        ):
+            copy = pltpu.make_async_remote_copy(
+                src_ref=src.at[block],
+                dst_ref=dst.at[block],
+                send_sem=send.at[step - 1],
+                recv_sem=recv.at[step - 1],
+                device_id=(target, col),
+                device_id_type=MESH,
+            )
+            copy.start()
+            pair.append(copy)
+        halos.append((block, pair))
+
+    def local_total(index):
+        block, pair = halos[index]
+        for copy in pair:
+            copy.wait_recv()
+        return (
+            mid_ref[block]
+            + from_down[block].astype(jnp.float32)
+            + from_up[block].astype(jnp.float32)
+        )
+
+    for step in range(1, n_col):
+        value = local_total(step - 1)
+        if step > 1:
+            value = value + ring_in[step - 2]
+        ring_out[step - 1] = value
+        copy = pltpu.make_async_remote_copy(
+            src_ref=ring_out.at[step - 1],
+            dst_ref=ring_in.at[step - 1],
+            send_sem=ring_send.at[step - 1],
+            recv_sem=ring_recv.at[step - 1],
+            device_id=(row, succ),
+            device_id_type=MESH,
+        )
+        copy.start()
+        copy.wait()
+    o_ref[...] = local_total(n_col - 1) + ring_in[n_col - 2]
+    for _, pair in halos:
+        for copy in pair:
+            copy.wait_send()
+
+
+def reduce_spread(mid, up_part, down_part, n_row, n_col):
+    _, rows, width = mid.shape
+    return pl.pallas_call(
+        functools.partial(spread_kernel, n_row, n_col),
+        out_shape=jax.ShapeDtypeStruct((rows, width), jnp.float32),
+        in_specs=[pl.BlockSpec(memory_space=pltpu.VMEM)] * 3,
+        out_specs=pl.BlockSpec(memory_space=pltpu.VMEM),
+        scratch_shapes=[
+            pltpu.VMEM((n_col, rows, width), up_part.dtype),
+            pltpu.VMEM((n_col, rows, width), up_part.dtype),
+            pltpu.VMEM((n_col - 1, rows, width), jnp.float32),
+            pltpu.VMEM((n_col - 1, rows, width), jnp.float32),
+            pltpu.SemaphoreType.DMA((n_col,)),
+            pltpu.SemaphoreType.DMA((n_col,)),
+            pltpu.SemaphoreType.DMA((n_col,)),
+            pltpu.SemaphoreType.DMA((n_col,)),
+            pltpu.SemaphoreType.DMA((n_col - 1,)),
+            pltpu.SemaphoreType.DMA((n_col - 1,)),
+        ],
+        compiler_params=pltpu.CompilerParams(collective_id=2, has_side_effects=True),
+    )(mid, up_part, down_part)
 
 
 def all_reduce(stacked, n_row, n_col):
@@ -270,12 +357,14 @@
     picked = grad_tiles[rows_part]
     products = jnp.einsum("tij,tif->tjf", tiles_part, picked, preferred_element_type=jnp.float32)
     spread = spread_zero.at[slot_cols].add(products * live_part[:, None, None])
-    spread = spread.reshape(3, col_count * node_rows, width)
-    middle = spread[1]
-    for offset in (1, -1):
-        outgoing = spread[2] if offset == 1 else spread[0]
-        middle = middle + passed_along(outgoing, "row", offset)
-    own_share = lax.psum_scatter(middle, "col", scatter_dimension=0, tiled=True)
+    spread = spread.reshape(3, col_count, node_rows, width)
+    own_share = reduce_spread(
+        spread[1],
+        spread[2].astype(jnp.bfloat16),
+        spread[0].astype(jnp.bfloat16),
+        row_count,
+        col_count,
+    )
     feature_grad = (own_share + self_feature).astype(jnp.bfloat16)
     summed_parts = all_reduce(
         jnp.concatenate([weight_part, self_part], axis=0), row_count, col_count

time: 298 us -> 258 us (0.87); the launches traced: 292 us -> 257 us
  waiting for transfers between devices: 97 us -> 0 us
  Pallas kernels: 127 us -> 215 us
  starting transfers between devices: 14.2 us -> 0 us
  between operations: 14.9 us -> 1.53 us
    ppermute x2 -> x0, waiting for transfers between devices: 97 us -> none  [passed_along(): return lax.ppermute(value, axis, pairs)]
    pallas_call x0 -> x1, Pallas kernels: none -> 86.1 us  [reduce_spread(): pl.pallas_call(functools.partial(spread_kernel, n_row, n_col), out_shape=...]
    ppermute x2 -> x0, starting transfers between devices: 14.1 us -> none  [passed_along(): return lax.ppermute(value, axis, pairs)]
    another operation x0 -> x1, other arithmetic: none -> 3.22 us
  transfers between devices with their start and end apart: 3 -> 0, of which waited for: 2 -> 0; matrix products, arithmetic and copies ran while one was open for 1% -> 0% of each run, Pallas kernels for 18% -> 0%
where the time goes in v3:
time: 258 us; the launch traced here: 257 us
  Pallas kernels  215 us (83%)
  local copies, waits for them, and re-layouts  17.6 us (7%)
  other arithmetic  16 us (6%)
  matrix products  7.28 us (3%)
    pallas_call x1, Pallas kernels, reduce_spread(): pl.pallas_call(functools.partial(spread_kernel, n_row, n_col), out_shape=...  86.1 us
    pallas_call x1, Pallas kernels, gather_window(): pl.pallas_call(functools.partial(gather_kernel, n_row, n_col), out_shape=...  74.2 us
    pallas_call x1, Pallas kernels, all_reduce(): pl.pallas_call(functools.partial(allreduce_kernel, n_row, n_col), out_sha...  54.7 us
    scatter-add x1, other arithmetic, shards(): spread = spread_zero.at[slot_cols].add(products * live_part[:, None, None])  10 us
    mul x1, local copies, waits for them, and re-layouts, shards(): spread = spread_zero.at[slot_cols].add(products * live_part[:, None, None])  5.58 us

profile of v3, /device:TPU:57, one launch (start us, length us, event | category | flops | bytes accessed | tf_op | source)
XLA Modules:
  0.0 257.5 jit_solution(643330116108393710)
XLA Ops:
  0.6 0.0 copy-start
  0.6 0.0 copy-start.8
  0.7 74.2 %shard_map.111 = bf16[3,8,256,256]{3,2,1,0:T(8,128)(2,1)} custom-call(bf16[256,256]{1,0:T(8,128)(2,1)} %x_ref.1), custom_call_target="tpu_custom_call" | custom-call | tf_op jit(solution)/shard_map/pallas_call | solution.py:162
  74.9 0.0 copy-done.8
  74.9 0.0 copy-start.9
  74.9 0.0 copy-start.1
  74.9 2.7 %gather_fusion = bf16[32,128,256]{2,1,0:T(8,128)(2,1)S(1)} fusion(bf16[48,128,256]{2,1,0:T(8,128)(2,1)} %bitcast.50, s32[1024]{0:T(1024)S(1)} %pad_clamp_fusion.1), kind=kCustom, calls=%fused_computation | custom fusion | bytes 4194432 | tf_op jit(solution)/shard_map/gather | solution.py:331
  78.3 0.0 copy-done.9
  78.3 0.0 copy-done.1
  78.3 0.0 copy-start.2
  78.3 0.0 copy-start.3
  78.3 0.0 copy-start.7
  78.3 0.8 fusion.9
  79.1 0.0 copy-start.5
  79.1 0.6 copy-done.5
  79.8 0.0 copy-done.2
  79.8 0.2 fusion.21
  79.9 0.0 copy-done
  80.0 0.0 copy-done.3
  80.0 0.0 copy-done.7
  80.0 0.9 multiply_convert_fusion
  80.9 0.2 convolution_convert_fusion
  81.2 0.7 gather_fusion.1
  81.9 2.9 %multiply_bitcast_fusion = f32[32,128,256]{1,2,0:T(8,128)} fusion(bf16[32,128,256]{2,1,0:T(8,128)(2,1)S(1)} %gather_fusion.1, f32[32]{0:T(128)S(1)} %get-tuple-element.11, bf16[1,32,128,128]{3,2,1,0:T(8,128)(2,1)S(1)} %copy-done.1), kind=kOutput, calls=%fused_computation.3 | convolution fusion | flops 269484032 | bytes 7340160 | tf_op jit(solution)/shard_map/tij,tif->tjf/dot_general | solution.py:358
  84.8 5.6 %copy.14 = f32[32,128,256]{2,1,0:T(8,128)} copy(f32[32,128,256]{1,2,0:T(8,128)} %multiply_bitcast_fusion) | data formatting | bytes 8388608 | tf_op jit(solution)/shard_map/mul | solution.py:359
  90.4 3.4 %broadcast_in_dim.2 = f32[48,128,256]{2,1,0:T(8,128)} broadcast(f32[]{:T(128)} %constant.3.clone.1), dimensions={} | broadcast | bytes 6291460 | tf_op jit(solution)/shard_map/broadcast_in_dim | solution.py:353
  93.8 10.0 %scatter_fusion = f32[48,128,256]{2,1,0:T(8,128)} fusion(f32[48,128,256]{2,1,0:T(8,128)} %broadcast_in_dim.2, s32[32]{0:T(128)S(1)} %fusion.16, f32[32,128,256]{2,1,0:T(8,128)} %copy.14), kind=kCustom, calls=%fused_computation.2 | custom fusion | flops 1048576 | bytes 12583040 | tf_op jit(solution)/shard_map/scatter-add | solution.py:359
  103.8 3.1 %slice.29 = f32[16,128,256]{2,1,0:T(8,128)} slice(f32[48,128,256]{2,1,0:T(8,128)} %scatter_fusion), slice={[16:32], [0:128], [0:256]} | slice | bytes 4194304 | tf_op jit(solution)/shard_map/slice | solution.py:362
  106.9 3.2 %convert.4 = bf16[48,128,256]{2,1,0:T(8,128)(2,1)S(1)} convert(f32[48,128,256]{2,1,0:T(8,128)} %scatter_fusion) | non-fusion elementwise | flops 1572864 | bytes 9437184 | tf_op jit(solution)/shard_map/convert.1
  110.2 1.5 fusion.20
  111.6 0.0 copy-start.4
  111.6 0.0 copy-start.6
  111.6 86.1 %shard_map.112 = f32[256,256]{1,0:T(8,128)} custom-call(f32[8,256,256]{2,1,0:T(8,128)} %bitcast.51, bf16[8,256,256]{2,1,0:T(8,128)(2,1)} %bitcast.53, bf16[8,256,256]{2,1,0:T(8,128)(2,1)} %bitcast.52), custom_call_target="tpu_custom_call" | custom-call | tf_op jit(solution)/shard_map/pallas_call | solution.py:246
  197.7 1.8 fusion.8
  199.6 0.0 copy-done.4
  199.6 0.2 convolution_bitcast_fusion
  199.8 0.0 copy-done.6
  199.8 0.2 fusion.22
  200.0 0.8 pad_maximum_fusion.x_ref
  200.9 54.7 %shard_map.113 = f32[512,256]{1,0:T(8,128)} custom-call(f32[512,256]{1,0:T(8,128)} %pad_maximum_fusion.x_ref), custom_call_target="tpu_custom_call" | custom-call | tf_op jit(solution)/shard_map/pallas_call | solution.py:271
  255.6 1.9 slice_multiply_fusion
  (6 shorter events, 0.0 us)
Async XLA Ops:
  0.6 79.3 %copy-start = (bf16[256,256]{1,0:T(8,128)(2,1)S(1)}, bf16[256,256]{1,0:T(8,128)(2,1)}, u32[]{:S(2)}) copy-start(bf16[256,256]{1,0:T(8,128)(2,1)} %param.10) | copy-start | bytes 393220
  0.6 74.2 %copy-start.8 = (s32[1,32]{1,0:T(1,128)S(1)}, s32[1,32]{1,0:T(1,128)}, u32[]{:S(2)}) copy-start(s32[1,32]{1,0:T(1,128)} %param.13) | copy-start | bytes 388
  74.9 3.4 %copy-start.9 = (s32[1,32]{1,0:T(1,128)S(1)}, s32[1,32]{1,0:T(1,128)}, u32[]{:S(2)}) copy-start(s32[1,32]{1,0:T(1,128)} %param.12) | copy-start | bytes 388
  74.9 3.4 %copy-start.1 = (bf16[1,32,128,128]{3,2,1,0:T(8,128)(2,1)S(1)}, bf16[1,32,128,128]{3,2,1,0:T(8,128)(2,1)}, u32[]{:S(2)}) copy-start(bf16[1,32,128,128]{3,2,1,0:T(8,128)(2,1)} %param.11) | copy-start | bytes 3145732
  78.3 1.5 copy-start.2
  78.3 1.6 copy-start.3
  78.3 1.6 copy-start.7
  79.1 0.7 copy-start.5
  111.6 87.9 %copy-start.4 = (bf16[256,256]{1,0:T(8,128)(2,1)S(1)}, bf16[256,256]{1,0:T(8,128)(2,1)}, u32[]{:S(2)}) copy-start(bf16[256,256]{1,0:T(8,128)(2,1)} %x_ref.1) | copy-start | bytes 393220
  111.6 88.2 %copy-start.6 = (bf16[2,128,256]{2,1,0:T(8,128)(2,1)S(1)}, bf16[2,128,256]{2,1,0:T(8,128)(2,1)}, u32[]{:S(2)}) copy-start(bf16[2,128,256]{2,1,0:T(8,128)(2,1)} %copy-done.5) | copy-start | bytes 393220

commit v4 on v3

--- a/solution.py
+++ b/solution.py
@@ -264,6 +264,86 @@
     )(mid, up_part, down_part)
 
 
+def local_kernel(rows_ref, cols_ref, count_ref, window_ref, tiles_ref, feat_ref, w_ref, ws_ref, cot_ref,
+                 act_ref, parts_ref, self_ref, mid_ref, up_ref, down_ref, acc, grad_agg, spread):
+    tile = tiles_ref.shape[-1]
+    nodes = acc.shape[0]
+    span = mid_ref.shape[0]
+    count = jnp.minimum(count_ref[0], tiles_ref.shape[0])
+    acc[...] = jnp.zeros_like(acc)
+
+    def forward(j, carry):
+        at = pl.multiple_of(rows_ref[j] * tile, tile)
+        acc[pl.ds(at, tile), :] += jnp.dot(
+            tiles_ref[j], window_ref[cols_ref[j]], preferred_element_type=jnp.float32
+        )
+        return carry
+
+    lax.fori_loop(0, count, forward, 0)
+    aggregated = acc[...].astype(jnp.bfloat16)
+    features = feat_ref[...]
+    pre_act = jnp.dot(aggregated, w_ref[...], preferred_element_type=jnp.float32) + jnp.dot(
+        features, ws_ref[...], preferred_element_type=jnp.float32
+    )
+    sigma = jax.nn.sigmoid(pre_act)
+    act_ref[...] = (pre_act * sigma).astype(act_ref.dtype)
+    grad_pre = (cot_ref[...].astype(jnp.float32) * sigma * (1.0 + pre_act * (1.0 - sigma))).astype(
+        jnp.bfloat16
+    )
+    over_nodes = (((0,), (0,)), ((), ()))
+    parts_ref[pl.ds(0, nodes), :] = lax.dot_general(
+        aggregated, grad_pre, over_nodes, preferred_element_type=jnp.float32
+    )
+    parts_ref[pl.ds(nodes, nodes), :] = lax.dot_general(
+        features, grad_pre, over_nodes, preferred_element_type=jnp.float32
+    )
+    by_rows = (((1,), (1,)), ((), ()))
+    grad_agg[...] = lax.dot_general(
+        grad_pre, w_ref[...], by_rows, preferred_element_type=jnp.float32
+    ).astype(jnp.bfloat16)
+    self_ref[...] = lax.dot_general(grad_pre, ws_ref[...], by_rows, preferred_element_type=jnp.float32)
+    spread[...] = jnp.zeros_like(spread)
+
+    def backward(j, carry):
+        at = pl.multiple_of(rows_ref[j] * tile, tile)
+        column = cols_ref[j]
+        spread[column] += lax.dot_general(
+            tiles_ref[j], grad_agg[pl.ds(at, tile), :], over_nodes, preferred_element_type=jnp.float32
+        )
+        return carry
+
+    lax.fori_loop(0, count, backward, 0)
+    mid_ref[...] = spread[pl.ds(span, span)]
+    up_ref[...] = spread[pl.ds(2 * span, span)].astype(up_ref.dtype)
+    down_ref[...] = spread[pl.ds(0, span)].astype(down_ref.dtype)
+
+
+def local_math(slot_rows, slot_cols, count, window, tiles, features, weight, weight_self, cotangent):
+    nodes, width = features.shape
+    span = window.shape[0] // 3
+    tile = tiles.shape[-1]
+    smem = pl.BlockSpec(memory_space=pltpu.SMEM)
+    vmem = pl.BlockSpec(memory_space=pltpu.VMEM)
+    return pl.pallas_call(
+        local_kernel,
+        out_shape=(
+            jax.ShapeDtypeStruct((nodes, width), jnp.bfloat16),
+            jax.ShapeDtypeStruct((2 * width, width), jnp.float32),
+            jax.ShapeDtypeStruct((nodes, width), jnp.float32),
+            jax.ShapeDtypeStruct((span, tile, width), jnp.float32),
+            jax.ShapeDtypeStruct((span, tile, width), jnp.bfloat16),
+            jax.ShapeDtypeStruct((span, tile, width), jnp.bfloat16),
+        ),
+        in_specs=[smem, smem, smem] + [vmem] * 6,
+        out_specs=(vmem,) * 6,
+        scratch_shapes=[
+            pltpu.VMEM((nodes, width), jnp.float32),
+            pltpu.VMEM((nodes, width), jnp.bfloat16),
+            pltpu.VMEM((3 * span, tile, width), jnp.float32),
+        ],
+    )(slot_rows, slot_cols, count, window, tiles, features, weight, weight_self, cotangent)
+
+
 def all_reduce(stacked, n_row, n_col):
     rows, width = stacked.shape
     col_bits = n_col.bit_length() - 1
@@ -324,51 +404,26 @@
     span = col_count * per_block
     window = gather_window(features, row_count, col_count)
     window_tiles = window.reshape(-1, tile_side, width)
-    row_ids = jnp.arange(per_block, dtype=jnp.int32)
-    tiles_part = tile_block
-    rows_part = slot_rows
-    live_part = jnp.arange(slot_total, dtype=jnp.int32) < live_count
-    feat_tiles = window_tiles[slot_cols]
-    selector = ((rows_part[None, :] == row_ids[:, None]) & live_part[None, :]).astype(jnp.bfloat16)
-    masked = tiles_part[None, :, :, :] * selector[:, :, None, None]
-    summed = jnp.einsum("ktij,tjf->kif", masked, feat_tiles, preferred_element_type=jnp.float32)
-    aggregated = summed.reshape(node_rows, width).astype(jnp.bfloat16)
-    pre_act = jnp.dot(aggregated, weight, preferred_element_type=jnp.float32) + jnp.dot(
-        features, weight_self, preferred_element_type=jnp.float32
-    )
-    activations = jax.nn.silu(pre_act).astype(jnp.bfloat16)
-    sigma = jax.nn.sigmoid(pre_act)
-    grad_pre = (cotangent.astype(jnp.float32) * sigma * (1.0 + pre_act * (1.0 - sigma))).astype(
-        jnp.bfloat16
-    )
-    weight_part = jnp.einsum("nf,ng->fg", aggregated, grad_pre, preferred_element_type=jnp.float32)
-    self_part = jnp.einsum("nf,ng->fg", features, grad_pre, preferred_element_type=jnp.float32)
-    grad_aggregated = jnp.einsum(
-        "ng,fg->nf", grad_pre, weight, preferred_element_type=jnp.float32
-    ).astype(jnp.bfloat16)
-    self_feature = jnp.einsum(
-        "ng,fg->nf", grad_pre, weight_self, preferred_element_type=jnp.float32
-    )
-    grad_tiles = grad_aggregated.reshape(per_block, tile_side, width)
-    spread_zero = jnp.zeros((3 * span, tile_side, width), jnp.float32)
-    tiles_part = tile_block
-    rows_part = slot_rows
-    live_part = (jnp.arange(slot_total, dtype=jnp.int32) < live_count).astype(jnp.float32)
-    picked = grad_tiles[rows_part]
-    products = jnp.einsum("tij,tif->tjf", tiles_part, picked, preferred_element_type=jnp.float32)
-    spread = spread_zero.at[slot_cols].add(products * live_part[:, None, None])
-    spread = spread.reshape(3, col_count, node_rows, width)
+    activations, parts, self_feature, mid, up_part, down_part = local_math(
+        slot_rows,
+        slot_cols,
+        tile_count[0],
+        window_tiles,
+        tile_block,
+        features,
+        weight,
+        weight_self,
+        cotangent,
+    )
     own_share = reduce_spread(
-        spread[1],
-        spread[2].astype(jnp.bfloat16),
-        spread[0].astype(jnp.bfloat16),
+        mid.reshape(col_count, node_rows, width),
+        up_part.reshape(col_count, node_rows, width),
+        down_part.reshape(col_count, node_rows, width),
         row_count,
         col_count,
     )
     feature_grad = (own_share + self_feature).astype(jnp.bfloat16)
-    summed_parts = all_reduce(
-        jnp.concatenate([weight_part, self_part], axis=0), row_count, col_count
-    )
+    summed_parts = all_reduce(parts, row_count, col_count)
     weight_total, self_total = summed_parts[:width], summed_parts[width:]
     factor = 1.0 / math.sqrt(node_rows * col_count * row_count)
     return (activations, feature_grad, weight_total * factor, self_total * factor)

time: 258 us -> 228 us (0.88)
  local copies, waits for them, and re-layouts: 17.6 us -> 0.01 us
  other arithmetic: 16 us -> 1.96 us
  Pallas kernels: 215 us -> 225 us
  matrix products: 7.28 us -> 0 us
    scatter-add x1 -> x0, other arithmetic: 10 us -> none  [shards(): spread = spread_zero.at[slot_cols].add(products * live_part[:, None, None])]
    dot_general x8 -> x0, matrix products: 7.28 us -> none  [the longest x1 2.91 us: shards(): jnp.einsum('tij,tif->tjf', tiles_part, picked, preferred_element_type=jnp...]
    pallas_call x0 -> x1, Pallas kernels: none -> 6.01 us  [local_math(): pl.pallas_call(local_kernel, out_shape=(jax.ShapeDtypeStruct((nodes, widt...]
    mul x1 -> x0, local copies, waits for them, and re-layouts: 5.58 us -> none  [shards(): spread = spread_zero.at[slot_cols].add(products * live_part[:, None, None])]
    slice x2 -> x0, local copies, waits for them, and re-layouts: 4.59 us -> none  [the longest x1 3.12 us: shards(): spread[1]]
    broadcast_in_dim x1 -> x0, local copies, waits for them, and re-layouts: 3.41 us -> none  [shards(): spread_zero = jnp.zeros((3 * span, tile_side, width), jnp.float32)]
    gather x2 -> x0, local copies, waits for them, and re-layouts: 3.34 us -> none  [the longest x1 2.66 us: shards(): feat_tiles = window_tiles[slot_cols]]
    another operation x1 -> x0, other arithmetic: 3.22 us -> none
where the time goes in v4:
time: 228 us
  Pallas kernels  225 us (99%)
    pallas_call x1, Pallas kernels, reduce_spread(): pl.pallas_call(functools.partial(spread_kernel, n_row, n_col), out_shape=...  88.3 us
    pallas_call x1, Pallas kernels, gather_window(): pl.pallas_call(functools.partial(gather_kernel, n_row, n_col), out_shape=...  74.1 us
    pallas_call x1, Pallas kernels, all_reduce(): pl.pallas_call(functools.partial(allreduce_kernel, n_row, n_col), out_sha...  56.3 us
    pallas_call x1, Pallas kernels, local_math(): pl.pallas_call(local_kernel, out_shape=(jax.ShapeDtypeStruct((nodes, widt...  6.01 us

profile of v4, /device:TPU:57, one launch (start us, length us, event | category | flops | bytes accessed | tf_op | source)
XLA Modules:
  0.0 228.0 jit_solution(5638411609510973558)
XLA Ops:
  1.3 74.1 %shard_map.111 = bf16[3,8,256,256]{3,2,1,0:T(8,128)(2,1)} custom-call(bf16[256,256]{1,0:T(8,128)(2,1)} %feat_ref.1), custom_call_target="tpu_custom_call" | custom-call | tf_op jit(solution)/shard_map/pallas_call | solution.py:162
  75.4 6.0 %shard_map.112 = (bf16[256,256]{1,0:T(8,128)(2,1)}, f32[512,256]{1,0:T(8,128)}, f32[256,256]{1,0:T(8,128)}, f32[16,128,256]{2,1,0:T(8,128)}, bf16[16,128,256]{2,...) custom-call(s32[32]{0:T(128)} %bitcast.14, s32[32]{0:T(128)} %bitcast.15, s32[1]{0:T(128)} %bitcast.8.count_ref, ...), custom_call_target="tpu_custom_call" | custom-call | tf_op jit(solution)/shard_map/pallas_call | solution.py:327
  81.4 0.0 copy-start
  81.4 88.3 %shard_map.113 = f32[256,256]{1,0:T(8,128)} custom-call(f32[8,256,256]{2,1,0:T(8,128)} %bitcast.10, bf16[8,256,256]{2,1,0:T(8,128)(2,1)} %bitcast.11, bf16[8,256,256]{2,1,0:T(8,128)(2,1)} %bitcast.12), custom_call_target="tpu_custom_call" | custom-call | tf_op jit(solution)/shard_map/pallas_call | solution.py:246
  169.8 56.3 %shard_map.114 = f32[512,256]{1,0:T(8,128)} custom-call(f32[512,256]{1,0:T(8,128)} %get-tuple-element.15.x_ref), custom_call_target="tpu_custom_call" | custom-call | tf_op jit(solution)/shard_map/pallas_call | solution.py:351
  226.1 0.0 copy-done
  226.1 2.0 slice_multiply_fusion
Async XLA Ops:
  81.4 144.6 %copy-start = (f32[256,256]{1,0:T(8,128)S(1)}, f32[256,256]{1,0:T(8,128)}, u32[]{:S(2)}) copy-start(f32[256,256]{1,0:T(8,128)} %get-tuple-element.14) | copy-start | bytes 786436

commit v5 on v4

--- a/solution.py
+++ b/solution.py
@@ -16,21 +16,18 @@
     return index + stride - 2 * stride * bit, bit
 
 
-def allreduce_kernel(n_row, n_col, x_ref, o_ref, part, gath, rsend, rrecv, dsend, drecv, gsend, grecv):
-    row = lax.axis_index("row")
-    col = lax.axis_index("col")
+def allreduce_partners(n_row, n_col, row, col):
+    partners = []
+    for k in range(n_col.bit_length() - 1):
+        partners.append((row, flip(col, 1 << k)[0]))
+    for k in range(n_row.bit_length() - 1):
+        partners.append((flip(row, 1 << k)[0], col))
+    return partners
+
+
+def allreduce_steps(n_row, n_col, row, col, x_ref, o_ref, part, gath, rsend, rrecv, dsend, drecv, gsend, grecv):
     col_bits = n_col.bit_length() - 1
     row_bits = n_row.bit_length() - 1
-    partners = []
-    for k in range(col_bits):
-        partners.append((row, flip(col, 1 << k)[0]))
-    for k in range(row_bits):
-        partners.append((flip(row, 1 << k)[0], col))
-    barrier = pltpu.get_barrier_semaphore()
-    for device in partners:
-        pl.semaphore_signal(barrier, inc=1, device_id=device, device_id_type=MESH)
-    pl.semaphore_wait(barrier, len(partners))
-
     rows = x_ref.shape[0]
     src = x_ref
     base = 0
@@ -49,7 +46,7 @@
             device_id_type=MESH,
         )
         copy.start()
-        copy.wait()
+        yield copy
         mine = src[pl.ds(pl.multiple_of(keep, 8), half), :] + part[k, pl.ds(0, half), :]
         gath[k, pl.ds(pl.multiple_of(keep, 8), half), :] = mine
         src = gath.at[k]
@@ -70,7 +67,7 @@
             device_id_type=MESH,
         )
         copy.start()
-        copy.wait()
+        yield copy
         total = total + part[col_bits + k, pl.ds(0, chunk), :]
     final = gath.at[col_bits]
     final[pl.ds(pl.multiple_of(base, 8), chunk), :] = total
@@ -87,10 +84,25 @@
             device_id_type=MESH,
         )
         copy.start()
-        copy.wait()
+        yield copy
         base = start
         size = size * 2
     o_ref[...] = final[...]
+
+
+def run_together(*chains):
+    active = list(chains)
+    while active:
+        copies, kept = [], []
+        for chain in active:
+            try:
+                copies.append(next(chain))
+                kept.append(chain)
+            except StopIteration:
+                pass
+        for copy in copies:
+            copy.wait()
+        active = kept
 
 
 def ring_position(col, n):
@@ -177,8 +189,9 @@
     )(block)
 
 
-def spread_kernel(n_row, n_col, mid_ref, up_ref, down_ref, o_ref, from_down, from_up, ring_in, ring_out,
-                  up_send, down_send, from_down_sem, from_up_sem, ring_send, ring_recv):
+def spread_kernel(n_row, n_col, mid_ref, up_ref, down_ref, parts_ref, o_ref, sums_ref, from_down, from_up,
+                  ring_in, ring_out, up_send, down_send, from_down_sem, from_up_sem, ring_send, ring_recv,
+                  part, gath, rsend, rrecv, dsend, drecv, gsend, grecv):
     row = lax.axis_index("row")
     col = lax.axis_index("col")
     p = ring_position(col, n_col)
@@ -186,10 +199,12 @@
     pred = ring_col((p + n_col - 1) % n_col, n_col)
     up = (row + 1) % n_row
     down = (row + n_row - 1) % n_row
+    partners = [(row, succ), (row, pred), (up, col), (down, col)]
+    partners += allreduce_partners(n_row, n_col, row, col)
     barrier = pltpu.get_barrier_semaphore()
-    for device in ((row, succ), (row, pred), (up, col), (down, col)):
+    for device in partners:
         pl.semaphore_signal(barrier, inc=1, device_id=device, device_id_type=MESH)
-    pl.semaphore_wait(barrier, 4)
+    pl.semaphore_wait(barrier, len(partners))
     halos = []
     for step in range(1, n_col + 1):
         block = ring_col((p - step + 2 * n_col) % n_col, n_col)
@@ -220,34 +235,47 @@
             + from_up[block].astype(jnp.float32)
         )
 
-    for step in range(1, n_col):
-        value = local_total(step - 1)
-        if step > 1:
-            value = value + ring_in[step - 2]
-        ring_out[step - 1] = value
-        copy = pltpu.make_async_remote_copy(
-            src_ref=ring_out.at[step - 1],
-            dst_ref=ring_in.at[step - 1],
-            send_sem=ring_send.at[step - 1],
-            recv_sem=ring_recv.at[step - 1],
-            device_id=(row, succ),
-            device_id_type=MESH,
-        )
-        copy.start()
-        copy.wait()
-    o_ref[...] = local_total(n_col - 1) + ring_in[n_col - 2]
+    def ring_steps():
+        for step in range(1, n_col):
+            value = local_total(step - 1)
+            if step > 1:
+                value = value + ring_in[step - 2]
+            ring_out[step - 1] = value
+            copy = pltpu.make_async_remote_copy(
+                src_ref=ring_out.at[step - 1],
+                dst_ref=ring_in.at[step - 1],
+                send_sem=ring_send.at[step - 1],
+                recv_sem=ring_recv.at[step - 1],
+                device_id=(row, succ),
+                device_id_type=MESH,
+            )
+            copy.start()
+            yield copy
+        o_ref[...] = local_total(n_col - 1) + ring_in[n_col - 2]
+
+    run_together(
+        allreduce_steps(n_row, n_col, row, col, parts_ref, sums_ref, part, gath,
+                        rsend, rrecv, dsend, drecv, gsend, grecv),
+        ring_steps(),
+    )
     for _, pair in halos:
         for copy in pair:
             copy.wait_send()
 
 
-def reduce_spread(mid, up_part, down_part, n_row, n_col):
+def reduce_spread(mid, up_part, down_part, parts, n_row, n_col):
     _, rows, width = mid.shape
+    col_bits = n_col.bit_length() - 1
+    row_bits = n_row.bit_length() - 1
+    stacked, _ = parts.shape
     return pl.pallas_call(
         functools.partial(spread_kernel, n_row, n_col),
-        out_shape=jax.ShapeDtypeStruct((rows, width), jnp.float32),
-        in_specs=[pl.BlockSpec(memory_space=pltpu.VMEM)] * 3,
-        out_specs=pl.BlockSpec(memory_space=pltpu.VMEM),
+        out_shape=(
+            jax.ShapeDtypeStruct((rows, width), jnp.float32),
+            jax.ShapeDtypeStruct(parts.shape, jnp.float32),
+        ),
+        in_specs=[pl.BlockSpec(memory_space=pltpu.VMEM)] * 4,
+        out_specs=(pl.BlockSpec(memory_space=pltpu.VMEM),) * 2,
         scratch_shapes=[
             pltpu.VMEM((n_col, rows, width), up_part.dtype),
             pltpu.VMEM((n_col, rows, width), up_part.dtype),
@@ -259,9 +287,17 @@
             pltpu.SemaphoreType.DMA((n_col,)),
             pltpu.SemaphoreType.DMA((n_col - 1,)),
             pltpu.SemaphoreType.DMA((n_col - 1,)),
+            pltpu.VMEM((col_bits + row_bits, stacked // 2, width), jnp.float32),
+            pltpu.VMEM((col_bits + 1, stacked, width), jnp.float32),
+            pltpu.SemaphoreType.DMA((col_bits,)),
+            pltpu.SemaphoreType.DMA((col_bits,)),
+            pltpu.SemaphoreType.DMA((row_bits,)),
+            pltpu.SemaphoreType.DMA((row_bits,)),
+            pltpu.SemaphoreType.DMA((col_bits,)),
+            pltpu.SemaphoreType.DMA((col_bits,)),
         ],
         compiler_params=pltpu.CompilerParams(collective_id=2, has_side_effects=True),
-    )(mid, up_part, down_part)
+    )(mid, up_part, down_part, parts)
 
 
 def local_kernel(rows_ref, cols_ref, count_ref, window_ref, tiles_ref, feat_ref, w_ref, ws_ref, cot_ref,
@@ -342,51 +378,6 @@
             pltpu.VMEM((3 * span, tile, width), jnp.float32),
         ],
     )(slot_rows, slot_cols, count, window, tiles, features, weight, weight_self, cotangent)
-
-
-def all_reduce(stacked, n_row, n_col):
-    rows, width = stacked.shape
-    col_bits = n_col.bit_length() - 1
-    row_bits = n_row.bit_length() - 1
-    return pl.pallas_call(
-        functools.partial(allreduce_kernel, n_row, n_col),
-        out_shape=jax.ShapeDtypeStruct((rows, width), jnp.float32),
-        in_specs=[pl.BlockSpec(memory_space=pltpu.VMEM)],
-        out_specs=pl.BlockSpec(memory_space=pltpu.VMEM),
-        scratch_shapes=[
-            pltpu.VMEM((col_bits + row_bits, rows // 2, width), jnp.float32),
-            pltpu.VMEM((col_bits + 1, rows, width), jnp.float32),
-            pltpu.SemaphoreType.DMA((col_bits,)),
-            pltpu.SemaphoreType.DMA((col_bits,)),
-            pltpu.SemaphoreType.DMA((row_bits,)),
-            pltpu.SemaphoreType.DMA((row_bits,)),
-            pltpu.SemaphoreType.DMA((col_bits,)),
-            pltpu.SemaphoreType.DMA((col_bits,)),
-        ],
-        compiler_params=pltpu.CompilerParams(collective_id=0, has_side_effects=True),
-    )(stacked)
-
-
-def with_halo(cells, sides, width):
-    for axis, dim in sides:
-        count = lax.axis_size(axis)
-        head = lax.slice_in_dim(cells, 0, width, axis=dim)
-        tail = lax.slice_in_dim(cells, cells.shape[dim] - width, cells.shape[dim], axis=dim)
-        cells = jnp.concatenate(
-            [
-                lax.ppermute(tail, axis, [(i, (i + 1) % count) for i in range(count)]),
-                cells,
-                lax.ppermute(head, axis, [((i + 1) % count, i) for i in range(count)]),
-            ],
-            axis=dim,
-        )
-    return cells
-
-
-def passed_along(value, axis, steps):
-    count = lax.axis_size(axis)
-    pairs = [(source, (source + steps) % count) for source in range(count)]
-    return lax.ppermute(value, axis, pairs)
 
 
 def shards(features, weight, weight_self, tile_values, tile_rows, tile_cols, tile_count, cotangent):
@@ -415,15 +406,15 @@
         weight_self,
         cotangent,
     )
-    own_share = reduce_spread(
+    own_share, summed_parts = reduce_spread(
         mid.reshape(col_count, node_rows, width),
         up_part.reshape(col_count, node_rows, width),
         down_part.reshape(col_count, node_rows, width),
+        parts,
         row_count,
         col_count,
     )
     feature_grad = (own_share + self_feature).astype(jnp.bfloat16)
-    summed_parts = all_reduce(parts, row_count, col_count)
     weight_total, self_total = summed_parts[:width], summed_parts[width:]
     factor = 1.0 / math.sqrt(node_rows * col_count * row_count)
     return (activations, feature_grad, weight_total * factor, self_total * factor)

time: 228 us -> 200 us (0.88)
  the two profiles are of different devices: /device:TPU:57 before, /device:TPU:67 now
where the time goes in v5:
time: 200 us
  Pallas kernels  197 us (98%)
    pallas_call x1, Pallas kernels, reduce_spread(): pl.pallas_call(functools.partial(spread_kernel, n_row, n_col), out_shape=...  145 us
    pallas_call x1, Pallas kernels, gather_window(): pl.pallas_call(functools.partial(gather_kernel, n_row, n_col), out_shape=...  37.8 us
    pallas_call x1, Pallas kernels, local_math(): pl.pallas_call(local_kernel, out_shape=(jax.ShapeDtypeStruct((nodes, widt...  13.7 us

profile of v5, /device:TPU:67, one launch (start us, length us, event | category | flops | bytes accessed | tf_op | source)
XLA Modules:
  0.0 200.0 jit_solution(11193115808446281463)
XLA Ops:
  1.3 37.8 %shard_map.111 = bf16[3,8,256,256]{3,2,1,0:T(8,128)(2,1)} custom-call(bf16[256,256]{1,0:T(8,128)(2,1)} %feat_ref.1), custom_call_target="tpu_custom_call" | custom-call | tf_op jit(solution)/shard_map/pallas_call | solution.py:174
  39.1 13.7 %shard_map.112 = (bf16[256,256]{1,0:T(8,128)(2,1)}, f32[512,256]{1,0:T(8,128)}, f32[256,256]{1,0:T(8,128)}, f32[16,128,256]{2,1,0:T(8,128)}, bf16[16,128,256]{2,...) custom-call(s32[32]{0:T(128)} %bitcast.14, s32[32]{0:T(128)} %bitcast.15, s32[1]{0:T(128)} %bitcast.8.count_ref, ...), custom_call_target="tpu_custom_call" | custom-call | tf_op jit(solution)/shard_map/pallas_call | solution.py:363
  52.8 0.0 copy-start
  52.8 145.2 %shard_map.113 = (f32[256,256]{1,0:T(8,128)}, f32[512,256]{1,0:T(8,128)}) custom-call(f32[8,256,256]{2,1,0:T(8,128)} %bitcast.10, bf16[8,256,256]{2,1,0:T(8,128)(2,1)} %bitcast.12, bf16[8,256,256]{2,1,0:T(8,128)(2,1)} %bitcast.13, f32[512,256]{1,0:T(8,128)} %get-tuple-element.16.parts_ref), custom_call_target="tpu_custom_call" | custom-call | tf_op jit(solution)/shard_map/pallas_call | solution.py:271
  198.0 0.0 copy-done
  198.0 2.0 slice_multiply_fusion
Async XLA Ops:
  52.8 145.2 %copy-start = (f32[256,256]{1,0:T(8,128)S(1)}, f32[256,256]{1,0:T(8,128)}, u32[]{:S(2)}) copy-start(f32[256,256]{1,0:T(8,128)} %get-tuple-element.18) | copy-start | bytes 786436

commit v6 on v5

--- a/solution.py
+++ b/solution.py
@@ -117,7 +117,7 @@
     return 2 * y + q
 
 
-def gather_kernel(n_row, n_col, x_ref, w_ref, ring_send, ring_recv, up_send, up_recv, down_send, down_recv, local_sem):
+def gather_kernel(n_row, n_col, x_ref, w_ref, ring_send, ring_recv, halo_send, halo_recv, local_sem):
     row = lax.axis_index("row")
     col = lax.axis_index("col")
     p = ring_position(col, n_col)
@@ -131,41 +131,40 @@
     pl.semaphore_wait(barrier, 4)
     local = pltpu.make_async_copy(x_ref, w_ref.at[1, col], local_sem.at[0])
     local.start()
-    halos = []
-
-    def halo(src, block, step):
-        for target, slot, send, recv in ((up, 0, up_send, up_recv), (down, 2, down_send, down_recv)):
+    halos = {}
+    for target, slot in ((up, 0), (down, 2)):
+        copy = pltpu.make_async_remote_copy(
+            src_ref=x_ref,
+            dst_ref=w_ref.at[slot, col],
+            send_sem=halo_send.at[slot // 2],
+            recv_sem=halo_recv.at[slot // 2],
+            device_id=(target, col),
+            device_id_type=MESH,
+        )
+        copy.start()
+        halos[slot] = copy
+    sent = col
+    for step in range(1, n_col):
+        copies = []
+        for group in (1, 0, 2):
+            if step == 1 and group != 1:
+                halos[group].wait_recv()
+            src = x_ref if (step == 1 and group == 1) else w_ref.at[group, sent]
             copy = pltpu.make_async_remote_copy(
                 src_ref=src,
-                dst_ref=w_ref.at[slot, block],
-                send_sem=send.at[step],
-                recv_sem=recv.at[step],
-                device_id=(target, col),
+                dst_ref=w_ref.at[group, sent],
+                send_sem=ring_send.at[group, step - 1],
+                recv_sem=ring_recv.at[group, step - 1],
+                device_id=(row, succ),
                 device_id_type=MESH,
             )
             copy.start()
-            halos.append(copy)
-
-    halo(x_ref, col, 0)
-    src = x_ref
-    sent = col
-    for step in range(1, n_col):
-        got = ring_col((p - step + n_col) % n_col, n_col)
-        copy = pltpu.make_async_remote_copy(
-            src_ref=src,
-            dst_ref=w_ref.at[1, sent],
-            send_sem=ring_send.at[step - 1],
-            recv_sem=ring_recv.at[step - 1],
-            device_id=(row, succ),
-            device_id_type=MESH,
-        )
-        copy.start()
-        copy.wait()
-        src = w_ref.at[1, got]
-        sent = got
-        halo(src, got, step)
-    for copy in halos:
-        copy.wait()
+            copies.append(copy)
+        for copy in copies:
+            copy.wait()
+        sent = ring_col((p - step + n_col) % n_col, n_col)
+    for copy in halos.values():
+        copy.wait_send()
     local.wait()
 
 
@@ -177,12 +176,10 @@
         in_specs=[pl.BlockSpec(memory_space=pltpu.VMEM)],
         out_specs=pl.BlockSpec(memory_space=pltpu.VMEM),
         scratch_shapes=[
-            pltpu.SemaphoreType.DMA((n_col - 1,)),
-            pltpu.SemaphoreType.DMA((n_col - 1,)),
-            pltpu.SemaphoreType.DMA((n_col,)),
-            pltpu.SemaphoreType.DMA((n_col,)),
-            pltpu.SemaphoreType.DMA((n_col,)),
-            pltpu.SemaphoreType.DMA((n_col,)),
+            pltpu.SemaphoreType.DMA((3, n_col - 1)),
+            pltpu.SemaphoreType.DMA((3, n_col - 1)),
+            pltpu.SemaphoreType.DMA((2,)),
+            pltpu.SemaphoreType.DMA((2,)),
             pltpu.SemaphoreType.DMA((1,)),
         ],
         compiler_params=pltpu.CompilerParams(collective_id=1, has_side_effects=True),

time: 200 us -> 186 us (0.930)
  the two profiles are of different devices: /device:TPU:67 before, /device:TPU:75 now
where the time goes in v6:
time: 186 us
  Pallas kernels  183 us (98%)
  other arithmetic  1.96 us (1%)
    pallas_call x1, Pallas kernels, reduce_spread(): pl.pallas_call(functools.partial(spread_kernel, n_row, n_col), out_shape=...  122 us
    pallas_call x1, Pallas kernels, gather_window(): pl.pallas_call(functools.partial(gather_kernel, n_row, n_col), out_shape=...  53.3 us
    pallas_call x1, Pallas kernels, local_math(): pl.pallas_call(local_kernel, out_shape=(jax.ShapeDtypeStruct((nodes, widt...  8.11 us

profile of v6, /device:TPU:75, one launch (start us, length us, event | category | flops | bytes accessed | tf_op | source)
XLA Modules:
  0.0 186.3 jit_solution(18906599912648364)
XLA Ops:
  1.3 53.3 %shard_map.111 = bf16[3,8,256,256]{3,2,1,0:T(8,128)(2,1)} custom-call(bf16[256,256]{1,0:T(8,128)(2,1)} %feat_ref.1), custom_call_target="tpu_custom_call" | custom-call | tf_op jit(solution)/shard_map/pallas_call | solution.py:173
  54.5 8.1 %shard_map.112 = (bf16[256,256]{1,0:T(8,128)(2,1)}, f32[512,256]{1,0:T(8,128)}, f32[256,256]{1,0:T(8,128)}, f32[16,128,256]{2,1,0:T(8,128)}, bf16[16,128,256]{2,...) custom-call(s32[32]{0:T(128)} %bitcast.14, s32[32]{0:T(128)} %bitcast.15, s32[1]{0:T(128)} %bitcast.8.count_ref, ...), custom_call_target="tpu_custom_call" | custom-call | tf_op jit(solution)/shard_map/pallas_call | solution.py:360
  62.7 0.0 copy-start
  62.7 121.7 %shard_map.113 = (f32[256,256]{1,0:T(8,128)}, f32[512,256]{1,0:T(8,128)}) custom-call(f32[8,256,256]{2,1,0:T(8,128)} %bitcast.10, bf16[8,256,256]{2,1,0:T(8,128)(2,1)} %bitcast.12, bf16[8,256,256]{2,1,0:T(8,128)(2,1)} %bitcast.13, f32[512,256]{1,0:T(8,128)} %get-tuple-element.16.parts_ref), custom_call_target="tpu_custom_call" | custom-call | tf_op jit(solution)/shard_map/pallas_call | solution.py:268
  184.3 0.0 copy-done
  184.4 2.0 %slice_multiply_fusion = (f32[256,256]{1,0:T(8,128)}, f32[256,256]{1,0:T(8,128)}, bf16[256,256]{1,0:T(8,128)(2,1)}) fusion(f32[512,256]{1,0:T(8,128)} %get-tuple-element.19, f32[256,256]{1,0:T(8,128)} %get-tuple-element.17, f32[256,256]{1,0:T(8,128)S(1)} %copy-done), kind=kLoop, calls=%fused_computation | loop fusion | flops 262144 | bytes 1703936 | tf_op jit(solution)/shard_map/mul | solution.py:417
Async XLA Ops:
  62.7 121.7 %copy-start = (f32[256,256]{1,0:T(8,128)S(1)}, f32[256,256]{1,0:T(8,128)}, u32[]{:S(2)}) copy-start(f32[256,256]{1,0:T(8,128)} %get-tuple-element.18) | copy-start | bytes 786436

commit v7 on v6

--- a/solution.py
+++ b/solution.py
@@ -125,32 +125,37 @@
     pred = ring_col((p + n_col - 1) % n_col, n_col)
     up = (row + 1) % n_row
     down = (row + n_row - 1) % n_row
+    half = max(n_row // 2, 1)
+    far = {0: row % half == 0, 2: (row + 1) % half == 0}
     barrier = pltpu.get_barrier_semaphore()
     for device in ((row, succ), (row, pred), (up, col), (down, col)):
         pl.semaphore_signal(barrier, inc=1, device_id=device, device_id_type=MESH)
     pl.semaphore_wait(barrier, 4)
     local = pltpu.make_async_copy(x_ref, w_ref.at[1, col], local_sem.at[0])
     local.start()
-    halos = {}
-    for target, slot in ((up, 0), (down, 2)):
-        copy = pltpu.make_async_remote_copy(
-            src_ref=x_ref,
-            dst_ref=w_ref.at[slot, col],
-            send_sem=halo_send.at[slot // 2],
-            recv_sem=halo_recv.at[slot // 2],
-            device_id=(target, col),
-            device_id_type=MESH,
-        )
+
+    def halo(src, block, index):
+        copies = {}
+        for target, slot in ((up, 0), (down, 2)):
+            copies[slot] = pltpu.make_async_remote_copy(
+                src_ref=src,
+                dst_ref=w_ref.at[slot, block],
+                send_sem=halo_send.at[slot // 2, index],
+                recv_sem=halo_recv.at[slot // 2, index],
+                device_id=(target, col),
+                device_id_type=MESH,
+            )
+        return copies
+
+    halos = [(col, halo(x_ref, col, 0))]
+    for copy in halos[0][1].values():
         copy.start()
-        halos[slot] = copy
     sent = col
     for step in range(1, n_col):
-        copies = []
+        copies = {}
         for group in (1, 0, 2):
-            if step == 1 and group != 1:
-                halos[group].wait_recv()
             src = x_ref if (step == 1 and group == 1) else w_ref.at[group, sent]
-            copy = pltpu.make_async_remote_copy(
+            copies[group] = pltpu.make_async_remote_copy(
                 src_ref=src,
                 dst_ref=w_ref.at[group, sent],
                 send_sem=ring_send.at[group, step - 1],
@@ -158,13 +163,40 @@
                 device_id=(row, succ),
                 device_id_type=MESH,
             )
-            copy.start()
-            copies.append(copy)
-        for copy in copies:
-            copy.wait()
+        copies[1].start()
+        for group in (0, 2):
+            @pl.when(far[group])
+            def _():
+                if step == 1:
+                    halos[0][1][group].wait_recv()
+                copies[group].start()
+        copies[1].wait()
+        for group in (0, 2):
+            @pl.when(far[group])
+            def _():
+                copies[group].wait()
         sent = ring_col((p - step + n_col) % n_col, n_col)
-    for copy in halos.values():
+        forward = halo(w_ref.at[1, sent], sent, step)
+        halos.append((sent, forward))
+        for slot in (0, 2):
+            @pl.when(jnp.logical_not(far[2 - slot]))
+            def _():
+                forward[slot].start()
+    for copy in halos[0][1].values():
         copy.wait_send()
+    for slot in (0, 2):
+        @pl.when(jnp.logical_not(far[slot]))
+        def _():
+            halos[0][1][slot].wait_recv()
+    for _, copies in halos[1:]:
+        for slot in (0, 2):
+            @pl.when(jnp.logical_not(far[2 - slot]))
+            def _():
+                copies[slot].wait_send()
+
+            @pl.when(jnp.logical_not(far[slot]))
+            def _():
+                copies[slot].wait_recv()
     local.wait()
 
 
@@ -178,8 +210,8 @@
         scratch_shapes=[
             pltpu.SemaphoreType.DMA((3, n_col - 1)),
             pltpu.SemaphoreType.DMA((3, n_col - 1)),
-            pltpu.SemaphoreType.DMA((2,)),
-            pltpu.SemaphoreType.DMA((2,)),
+            pltpu.SemaphoreType.DMA((2, n_col)),
+            pltpu.SemaphoreType.DMA((2, n_col)),
             pltpu.SemaphoreType.DMA((1,)),
         ],
         compiler_params=pltpu.CompilerParams(collective_id=1, has_side_effects=True),

time: 186 us -> 183 us (0.984)
  the two profiles are of different devices: /device:TPU:75 before, /device:TPU:11 now
where the time goes in v7:
time: 183 us
  Pallas kernels  180 us (98%)
  other arithmetic  1.96 us (1%)
    pallas_call x1, Pallas kernels, reduce_spread(): pl.pallas_call(functools.partial(spread_kernel, n_row, n_col), out_shape=...  134 us
    pallas_call x1, Pallas kernels, gather_window(): pl.pallas_call(functools.partial(gather_kernel, n_row, n_col), out_shape=...  39.8 us
    pallas_call x1, Pallas kernels, local_math(): pl.pallas_call(local_kernel, out_shape=(jax.ShapeDtypeStruct((nodes, widt...  6 us

profile of v7, /device:TPU:11, one launch (start us, length us, event | category | flops | bytes accessed | tf_op | source)
XLA Modules:
  0.0 183.1 jit_solution(12400764718908998026)
XLA Ops:
  1.3 39.8 %shard_map.111 = bf16[3,8,256,256]{3,2,1,0:T(8,128)(2,1)} custom-call(bf16[256,256]{1,0:T(8,128)(2,1)} %feat_ref.1), custom_call_target="tpu_custom_call" | custom-call | tf_op jit(solution)/shard_map/pallas_call | solution.py:205
  41.1 6.0 %shard_map.112 = (bf16[256,256]{1,0:T(8,128)(2,1)}, f32[512,256]{1,0:T(8,128)}, f32[256,256]{1,0:T(8,128)}, f32[16,128,256]{2,1,0:T(8,128)}, bf16[16,128,256]{2,...) custom-call(s32[32]{0:T(128)} %bitcast.14, s32[32]{0:T(128)} %bitcast.15, s32[1]{0:T(128)} %bitcast.8.count_ref, ...), custom_call_target="tpu_custom_call" | custom-call | tf_op jit(solution)/shard_map/pallas_call | solution.py:392
  47.1 0.0 copy-start
  47.1 134.0 %shard_map.113 = (f32[256,256]{1,0:T(8,128)}, f32[512,256]{1,0:T(8,128)}) custom-call(f32[8,256,256]{2,1,0:T(8,128)} %bitcast.10, bf16[8,256,256]{2,1,0:T(8,128)(2,1)} %bitcast.12, bf16[8,256,256]{2,1,0:T(8,128)(2,1)} %bitcast.13, f32[512,256]{1,0:T(8,128)} %get-tuple-element.16.parts_ref), custom_call_target="tpu_custom_call" | custom-call | tf_op jit(solution)/shard_map/pallas_call | solution.py:300
  181.1 0.0 copy-done
  181.1 2.0 %slice_multiply_fusion = (f32[256,256]{1,0:T(8,128)}, f32[256,256]{1,0:T(8,128)}, bf16[256,256]{1,0:T(8,128)(2,1)}) fusion(f32[512,256]{1,0:T(8,128)} %get-tuple-element.19, f32[256,256]{1,0:T(8,128)} %get-tuple-element.17, f32[256,256]{1,0:T(8,128)S(1)} %copy-done), kind=kLoop, calls=%fused_computation | loop fusion | flops 262144 | bytes 1703936 | tf_op jit(solution)/shard_map/mul | solution.py:449
Async XLA Ops:
  47.1 134.0 %copy-start = (f32[256,256]{1,0:T(8,128)S(1)}, f32[256,256]{1,0:T(8,128)}, u32[]{:S(2)}) copy-start(f32[256,256]{1,0:T(8,128)} %get-tuple-element.18) | copy-start | bytes 786436

commit v8 on v7

--- a/solution.py
+++ b/solution.py
@@ -218,8 +218,18 @@
     )(block)
 
 
-def spread_kernel(n_row, n_col, mid_ref, up_ref, down_ref, parts_ref, o_ref, sums_ref, from_down, from_up,
-                  ring_in, ring_out, up_send, down_send, from_down_sem, from_up_sem, ring_send, ring_recv,
+class Gated:
+    def __init__(self, copy, cond):
+        self.copy = copy
+        self.cond = cond
+
+    def wait(self):
+        pl.when(self.cond)(self.copy.wait)
+
+
+def spread_kernel(n_row, n_col, mid_ref, up_ref, down_ref, parts_ref, o_ref, sums_ref, up_bf, down_bf,
+                  from_down, from_up, ring_in, ring_out, far_in, far_out, far_from, up_send, down_send,
+                  from_down_sem, from_up_sem, ring_send, ring_recv, far_send, far_recv, last_send, last_recv,
                   part, gath, rsend, rrecv, dsend, drecv, gsend, grecv):
     row = lax.axis_index("row")
     col = lax.axis_index("col")
@@ -228,19 +238,24 @@
     pred = ring_col((p + n_col - 1) % n_col, n_col)
     up = (row + 1) % n_row
     down = (row + n_row - 1) % n_row
+    half = max(n_row // 2, 1)
+    far_down = row % half == 0
+    far_up = (row + 1) % half == 0
     partners = [(row, succ), (row, pred), (up, col), (down, col)]
     partners += allreduce_partners(n_row, n_col, row, col)
     barrier = pltpu.get_barrier_semaphore()
     for device in partners:
         pl.semaphore_signal(barrier, inc=1, device_id=device, device_id_type=MESH)
     pl.semaphore_wait(barrier, len(partners))
+    up_bf[...] = up_ref[...].astype(up_bf.dtype)
+    down_bf[...] = down_ref[...].astype(down_bf.dtype)
     halos = []
     for step in range(1, n_col + 1):
         block = ring_col((p - step + 2 * n_col) % n_col, n_col)
         pair = []
-        for src, dst, target, send, recv in (
-            (up_ref, from_down, up, up_send, from_down_sem),
-            (down_ref, from_up, down, down_send, from_up_sem),
+        for src, dst, target, send, recv, far in (
+            (up_bf, from_down, up, up_send, from_down_sem, far_up),
+            (down_bf, from_up, down, down_send, from_up_sem, far_down),
         ):
             copy = pltpu.make_async_remote_copy(
                 src_ref=src.at[block],
@@ -250,18 +265,19 @@
                 device_id=(target, col),
                 device_id_type=MESH,
             )
-            copy.start()
+            pl.when(jnp.logical_not(far))(copy.start)
             pair.append(copy)
         halos.append((block, pair))
 
     def local_total(index):
-        block, pair = halos[index]
-        for copy in pair:
-            copy.wait_recv()
+        block, (from_below, from_above) = halos[index]
+        pl.when(jnp.logical_not(far_down))(from_below.wait_recv)
+        pl.when(jnp.logical_not(far_up))(from_above.wait_recv)
+        zero = jnp.zeros(mid_ref.shape[1:], jnp.float32)
         return (
             mid_ref[block]
-            + from_down[block].astype(jnp.float32)
-            + from_up[block].astype(jnp.float32)
+            + jnp.where(far_down, zero, from_down[block].astype(jnp.float32))
+            + jnp.where(far_up, zero, from_up[block].astype(jnp.float32))
         )
 
     def ring_steps():
@@ -282,14 +298,65 @@
             yield copy
         o_ref[...] = local_total(n_col - 1) + ring_in[n_col - 2]
 
+    def far_steps(side, part_ref, far):
+        for step in range(1, n_col):
+            block = ring_col((p - step + 2 * n_col) % n_col, n_col)
+            copy = pltpu.make_async_remote_copy(
+                src_ref=far_out.at[side, step - 1],
+                dst_ref=far_in.at[side, step - 1],
+                send_sem=far_send.at[side, step - 1],
+                recv_sem=far_recv.at[side, step - 1],
+                device_id=(row, succ),
+                device_id_type=MESH,
+            )
+
+            def send(step=step, block=block, copy=copy):
+                value = part_ref[block]
+                if step > 1:
+                    value = value + far_in[side, step - 2]
+                far_out[side, step - 1] = value
+                copy.start()
+
+            pl.when(far)(send)
+            yield Gated(copy, far)
+
+        def finish():
+            far_out[side, n_col - 1] = part_ref[col] + far_in[side, n_col - 2]
+
+        pl.when(far)(finish)
+
     run_together(
         allreduce_steps(n_row, n_col, row, col, parts_ref, sums_ref, part, gath,
                         rsend, rrecv, dsend, drecv, gsend, grecv),
         ring_steps(),
-    )
-    for _, pair in halos:
-        for copy in pair:
-            copy.wait_send()
+        far_steps(0, up_ref, far_up),
+        far_steps(1, down_ref, far_down),
+    )
+    lasts = []
+    for side, target, slot, far in ((0, up, 0, far_up), (1, down, 1, far_down)):
+        copy = pltpu.make_async_remote_copy(
+            src_ref=far_out.at[side, n_col - 1],
+            dst_ref=far_from.at[slot],
+            send_sem=last_send.at[side],
+            recv_sem=last_recv.at[slot],
+            device_id=(target, col),
+            device_id_type=MESH,
+        )
+        pl.when(far)(copy.start)
+        lasts.append(copy)
+    pl.when(far_up)(lasts[0].wait_send)
+    pl.when(far_down)(lasts[1].wait_send)
+    pl.when(far_down)(lasts[0].wait_recv)
+    pl.when(far_up)(lasts[1].wait_recv)
+    zero = jnp.zeros(o_ref.shape, jnp.float32)
+    o_ref[...] = (
+        o_ref[...]
+        + jnp.where(far_down, far_from[0], zero)
+        + jnp.where(far_up, far_from[1], zero)
+    )
+    for _, (to_up, to_down) in halos:
+        pl.when(jnp.logical_not(far_up))(to_up.wait_send)
+        pl.when(jnp.logical_not(far_down))(to_down.wait_send)
 
 
 def reduce_spread(mid, up_part, down_part, parts, n_row, n_col):
@@ -306,16 +373,25 @@
         in_specs=[pl.BlockSpec(memory_space=pltpu.VMEM)] * 4,
         out_specs=(pl.BlockSpec(memory_space=pltpu.VMEM),) * 2,
         scratch_shapes=[
-            pltpu.VMEM((n_col, rows, width), up_part.dtype),
-            pltpu.VMEM((n_col, rows, width), up_part.dtype),
+            pltpu.VMEM((n_col, rows, width), jnp.bfloat16),
+            pltpu.VMEM((n_col, rows, width), jnp.bfloat16),
+            pltpu.VMEM((n_col, rows, width), jnp.bfloat16),
+            pltpu.VMEM((n_col, rows, width), jnp.bfloat16),
             pltpu.VMEM((n_col - 1, rows, width), jnp.float32),
             pltpu.VMEM((n_col - 1, rows, width), jnp.float32),
+            pltpu.VMEM((2, n_col - 1, rows, width), jnp.float32),
+            pltpu.VMEM((2, n_col, rows, width), jnp.float32),
+            pltpu.VMEM((2, rows, width), jnp.float32),
             pltpu.SemaphoreType.DMA((n_col,)),
             pltpu.SemaphoreType.DMA((n_col,)),
             pltpu.SemaphoreType.DMA((n_col,)),
             pltpu.SemaphoreType.DMA((n_col,)),
             pltpu.SemaphoreType.DMA((n_col - 1,)),
             pltpu.SemaphoreType.DMA((n_col - 1,)),
+            pltpu.SemaphoreType.DMA((2, n_col - 1)),
+            pltpu.SemaphoreType.DMA((2, n_col - 1)),
+            pltpu.SemaphoreType.DMA((2,)),
+            pltpu.SemaphoreType.DMA((2,)),
             pltpu.VMEM((col_bits + row_bits, stacked // 2, width), jnp.float32),
             pltpu.VMEM((col_bits + 1, stacked, width), jnp.float32),
             pltpu.SemaphoreType.DMA((col_bits,)),
@@ -396,8 +472,8 @@
             jax.ShapeDtypeStruct((2 * width, width), jnp.float32),
             jax.ShapeDtypeStruct((nodes, width), jnp.float32),
             jax.ShapeDtypeStruct((span, tile, width), jnp.float32),
-            jax.ShapeDtypeStruct((span, tile, width), jnp.bfloat16),
-            jax.ShapeDtypeStruct((span, tile, width), jnp.bfloat16),
+            jax.ShapeDtypeStruct((span, tile, width), jnp.float32),
+            jax.ShapeDtypeStruct((span, tile, width), jnp.float32),
         ),
         in_specs=[smem, smem, smem] + [vmem] * 6,
         out_specs=(vmem,) * 6,

time: 183 us -> 183 us (level)
  the two profiles are of different devices: /device:TPU:11 before, /device:TPU:1 now
where the time goes in v8:
time: 183 us
  Pallas kernels  179 us (98%)
  other arithmetic  1.96 us (1%)
    pallas_call x1, Pallas kernels, reduce_spread(): pl.pallas_call(functools.partial(spread_kernel, n_row, n_col), out_shape=...  109 us
    pallas_call x1, Pallas kernels, gather_window(): pl.pallas_call(functools.partial(gather_kernel, n_row, n_col), out_shape=...  60 us
    pallas_call x1, Pallas kernels, local_math(): pl.pallas_call(local_kernel, out_shape=(jax.ShapeDtypeStruct((nodes, widt...  11 us

profile of v8, /device:TPU:1, one launch (start us, length us, event | category | flops | bytes accessed | tf_op | source)
XLA Modules:
  0.0 182.7 jit_solution(6068951884306332513)
XLA Ops:
  1.3 60.0 %shard_map.111 = bf16[3,8,256,256]{3,2,1,0:T(8,128)(2,1)} custom-call(bf16[256,256]{1,0:T(8,128)(2,1)} %feat_ref.1), custom_call_target="tpu_custom_call" | custom-call | tf_op jit(solution)/shard_map/pallas_call | solution.py:205
  61.2 11.0 %shard_map.112 = (bf16[256,256]{1,0:T(8,128)(2,1)}, f32[512,256]{1,0:T(8,128)}, f32[256,256]{1,0:T(8,128)}, f32[16,128,256]{2,1,0:T(8,128)}, f32[16,128,256]{2,1,0:T(8,128)}, /*index=5*/f32[16,128,256]{2,1,0:T(8,128)}) custom-call(s32[32]{0:T(128)} %bitcast.14, s32[32]{0:T(128)} %bitcast.15, s32[1]{0:T(128)} %bitcast.8.count_ref, ...), custom_call_target="tpu_custom_call" | custom-call | tf_op jit(solution)/shard_map/pallas_call | solution.py:468
  72.2 0.0 copy-start
  72.2 108.5 %shard_map.113 = (f32[256,256]{1,0:T(8,128)}, f32[512,256]{1,0:T(8,128)}) custom-call(f32[8,256,256]{2,1,0:T(8,128)} %bitcast.10, f32[8,256,256]{2,1,0:T(8,128)} %bitcast.11, f32[8,256,256]{2,1,0:T(8,128)} %bitcast.12, f32[512,256]{1,0:T(8,128)} %get-tuple-element.16.parts_ref), custom_call_target="tpu_custom_call" | custom-call | tf_op jit(solution)/shard_map/pallas_call | solution.py:367
  180.8 0.0 copy-done
  180.8 2.0 %slice_multiply_fusion = (f32[256,256]{1,0:T(8,128)}, f32[256,256]{1,0:T(8,128)}, bf16[256,256]{1,0:T(8,128)(2,1)}) fusion(f32[512,256]{1,0:T(8,128)} %get-tuple-element.19, f32[256,256]{1,0:T(8,128)} %get-tuple-element.17, f32[256,256]{1,0:T(8,128)S(1)} %copy-done), kind=kLoop, calls=%fused_computation | loop fusion | flops 262144 | bytes 1703936 | tf_op jit(solution)/shard_map/mul | solution.py:525
Async XLA Ops:
  72.2 108.5 %copy-start = (f32[256,256]{1,0:T(8,128)S(1)}, f32[256,256]{1,0:T(8,128)}, u32[]{:S(2)}) copy-start(f32[256,256]{1,0:T(8,128)} %get-tuple-element.18) | copy-start | bytes 786436

commit v9 on v8

--- a/solution.py
+++ b/solution.py
@@ -17,50 +17,60 @@
 
 
 def allreduce_partners(n_row, n_col, row, col):
-    partners = []
-    for k in range(n_col.bit_length() - 1):
-        partners.append((row, flip(col, 1 << k)[0]))
+    partners = [(row, peer) for peer in range(n_col)]
     for k in range(n_row.bit_length() - 1):
         partners.append((flip(row, 1 << k)[0], col))
     return partners
 
 
+class Group:
+    def __init__(self, copies, receipts, col):
+        self.copies = copies
+        self.receipts = receipts
+        self.col = col
+
+    def wait(self):
+        for peer, (copy, receipt) in enumerate(zip(self.copies, self.receipts)):
+            @pl.when(peer != self.col)
+            def _():
+                copy.wait_send()
+                receipt.wait_recv()
+
+
 def allreduce_steps(n_row, n_col, row, col, x_ref, o_ref, part, gath, rsend, rrecv, dsend, drecv, gsend, grecv):
-    col_bits = n_col.bit_length() - 1
     row_bits = n_row.bit_length() - 1
-    rows = x_ref.shape[0]
-    src = x_ref
-    base = 0
-    size = rows
-    for k in range(col_bits):
-        other, bit = flip(col, 1 << k)
-        half = size // 2
-        keep = base + bit * half
-        give = base + (1 - bit) * half
-        copy = pltpu.make_async_remote_copy(
-            src_ref=src.at[pl.ds(pl.multiple_of(give, 8), half)],
-            dst_ref=part.at[k, pl.ds(0, half)],
-            send_sem=rsend.at[k],
-            recv_sem=rrecv.at[k],
-            device_id=(row, other),
+    chunk = x_ref.shape[0] // n_col
+    mine = pl.ds(pl.multiple_of(col * chunk, 8), chunk)
+    copies, receipts = [], []
+    for peer in range(n_col):
+        copies.append(pltpu.make_async_remote_copy(
+            src_ref=x_ref.at[pl.ds(peer * chunk, chunk)],
+            dst_ref=gath.at[0, col],
+            send_sem=rsend.at[peer],
+            recv_sem=rrecv.at[col],
+            device_id=(row, peer),
             device_id_type=MESH,
-        )
-        copy.start()
-        yield copy
-        mine = src[pl.ds(pl.multiple_of(keep, 8), half), :] + part[k, pl.ds(0, half), :]
-        gath[k, pl.ds(pl.multiple_of(keep, 8), half), :] = mine
-        src = gath.at[k]
-        base = keep
-        size = half
-    chunk = size
-    total = gath[col_bits - 1, pl.ds(pl.multiple_of(base, 8), chunk), :]
+        ))
+        receipts.append(pltpu.make_async_remote_copy(
+            src_ref=x_ref.at[pl.ds(peer * chunk, chunk)],
+            dst_ref=gath.at[0, peer],
+            send_sem=rsend.at[peer],
+            recv_sem=rrecv.at[peer],
+            device_id=(row, peer),
+            device_id_type=MESH,
+        ))
+        pl.when(peer != col)(copies[-1].start)
+    yield Group(copies, receipts, col)
+    total = x_ref[mine, :]
+    for peer in range(n_col):
+        total = total + jnp.where(peer == col, jnp.zeros_like(total), gath[0, peer])
     for k in range(row_bits):
         other, _ = flip(row, 1 << k)
-        hold = o_ref.at[pl.ds(0, chunk)]
+        hold = part.at[2 * k]
         hold[...] = total
         copy = pltpu.make_async_remote_copy(
             src_ref=hold,
-            dst_ref=part.at[col_bits + k, pl.ds(0, chunk)],
+            dst_ref=part.at[2 * k + 1],
             send_sem=dsend.at[k],
             recv_sem=drecv.at[k],
             device_id=(other, col),
@@ -68,26 +78,28 @@
         )
         copy.start()
         yield copy
-        total = total + part[col_bits + k, pl.ds(0, chunk), :]
-    final = gath.at[col_bits]
-    final[pl.ds(pl.multiple_of(base, 8), chunk), :] = total
-    size = chunk
-    for k in reversed(range(col_bits)):
-        other, bit = flip(col, 1 << k)
-        start = base - bit * size
-        copy = pltpu.make_async_remote_copy(
-            src_ref=final.at[pl.ds(pl.multiple_of(base, 8), size)],
-            dst_ref=final.at[pl.ds(pl.multiple_of(base, 8), size)],
-            send_sem=gsend.at[k],
-            recv_sem=grecv.at[k],
-            device_id=(row, other),
+        total = total + part[2 * k + 1]
+    o_ref[mine, :] = total
+    copies, receipts = [], []
+    for peer in range(n_col):
+        copies.append(pltpu.make_async_remote_copy(
+            src_ref=o_ref.at[mine],
+            dst_ref=o_ref.at[mine],
+            send_sem=gsend.at[peer],
+            recv_sem=grecv.at[col],
+            device_id=(row, peer),
             device_id_type=MESH,
-        )
-        copy.start()
-        yield copy
-        base = start
-        size = size * 2
-    o_ref[...] = final[...]
+        ))
+        receipts.append(pltpu.make_async_remote_copy(
+            src_ref=o_ref.at[mine],
+            dst_ref=o_ref.at[pl.ds(peer * chunk, chunk)],
+            send_sem=gsend.at[peer],
+            recv_sem=grecv.at[peer],
+            device_id=(row, peer),
+            device_id_type=MESH,
+        ))
+        pl.when(peer != col)(copies[-1].start)
+    yield Group(copies, receipts, col)
 
 
 def run_together(*chains):
@@ -245,8 +257,11 @@
     partners += allreduce_partners(n_row, n_col, row, col)
     barrier = pltpu.get_barrier_semaphore()
     for device in partners:
-        pl.semaphore_signal(barrier, inc=1, device_id=device, device_id_type=MESH)
-    pl.semaphore_wait(barrier, len(partners))
+        def signal(device=device):
+            pl.semaphore_signal(barrier, inc=1, device_id=device, device_id_type=MESH)
+
+        pl.when(jnp.logical_or(device[0] != row, device[1] != col))(signal)
+    pl.semaphore_wait(barrier, len(partners) - 1)
     up_bf[...] = up_ref[...].astype(up_bf.dtype)
     down_bf[...] = down_ref[...].astype(down_bf.dtype)
     halos = []
@@ -392,14 +407,14 @@
             pltpu.SemaphoreType.DMA((2, n_col - 1)),
             pltpu.SemaphoreType.DMA((2,)),
             pltpu.SemaphoreType.DMA((2,)),
-            pltpu.VMEM((col_bits + row_bits, stacked // 2, width), jnp.float32),
-            pltpu.VMEM((col_bits + 1, stacked, width), jnp.float32),
-            pltpu.SemaphoreType.DMA((col_bits,)),
-            pltpu.SemaphoreType.DMA((col_bits,)),
+            pltpu.VMEM((2 * row_bits, stacked // n_col, width), jnp.float32),
+            pltpu.VMEM((1, n_col, stacked // n_col, width), jnp.float32),
+            pltpu.SemaphoreType.DMA((n_col,)),
+            pltpu.SemaphoreType.DMA((n_col,)),
             pltpu.SemaphoreType.DMA((row_bits,)),
             pltpu.SemaphoreType.DMA((row_bits,)),
-            pltpu.SemaphoreType.DMA((col_bits,)),
-            pltpu.SemaphoreType.DMA((col_bits,)),
+            pltpu.SemaphoreType.DMA((n_col,)),
+            pltpu.SemaphoreType.DMA((n_col,)),
         ],
         compiler_params=pltpu.CompilerParams(collective_id=2, has_side_effects=True),
     )(mid, up_part, down_part, parts)

time: 183 us -> 187 us (1.022)
  the two profiles are of different devices: /device:TPU:1 before, /device:TPU:9 now
where the time goes in v9:
time: 187 us
  Pallas kernels  184 us (98%)
  other arithmetic  1.96 us (1%)
    pallas_call x1, Pallas kernels, reduce_spread(): pl.pallas_call(functools.partial(spread_kernel, n_row, n_col), out_shape=...  119 us
    pallas_call x1, Pallas kernels, gather_window(): pl.pallas_call(functools.partial(gather_kernel, n_row, n_col), out_shape=...  57.7 us
    pallas_call x1, Pallas kernels, local_math(): pl.pallas_call(local_kernel, out_shape=(jax.ShapeDtypeStruct((nodes, widt...  6.78 us

profile of v9, /device:TPU:9, one launch (start us, length us, event | category | flops | bytes accessed | tf_op | source)
XLA Modules:
  0.0 187.0 jit_solution(9447077914077779071)
XLA Ops:
  1.3 57.7 %shard_map.111 = bf16[3,8,256,256]{3,2,1,0:T(8,128)(2,1)} custom-call(bf16[256,256]{1,0:T(8,128)(2,1)} %feat_ref.1), custom_call_target="tpu_custom_call" | custom-call | tf_op jit(solution)/shard_map/pallas_call | solution.py:217
  59.0 6.8 %shard_map.112 = (bf16[256,256]{1,0:T(8,128)(2,1)}, f32[512,256]{1,0:T(8,128)}, f32[256,256]{1,0:T(8,128)}, f32[16,128,256]{2,1,0:T(8,128)}, f32[16,128,256]{2,1,0:T(8,128)}, /*index=5*/f32[16,128,256]{2,1,0:T(8,128)}) custom-call(s32[32]{0:T(128)} %bitcast.14, s32[32]{0:T(128)} %bitcast.15, s32[1]{0:T(128)} %bitcast.8.count_ref, ...), custom_call_target="tpu_custom_call" | custom-call | tf_op jit(solution)/shard_map/pallas_call | solution.py:483
  65.7 0.0 copy-start
  65.7 119.3 %shard_map.113 = (f32[256,256]{1,0:T(8,128)}, f32[512,256]{1,0:T(8,128)}) custom-call(f32[8,256,256]{2,1,0:T(8,128)} %bitcast.10, f32[8,256,256]{2,1,0:T(8,128)} %bitcast.11, f32[8,256,256]{2,1,0:T(8,128)} %bitcast.12, f32[512,256]{1,0:T(8,128)} %get-tuple-element.16.parts_ref), custom_call_target="tpu_custom_call" | custom-call | tf_op jit(solution)/shard_map/pallas_call | solution.py:382
  185.0 0.0 copy-done
  185.1 2.0 %slice_multiply_fusion = (f32[256,256]{1,0:T(8,128)}, f32[256,256]{1,0:T(8,128)}, bf16[256,256]{1,0:T(8,128)(2,1)}) fusion(f32[512,256]{1,0:T(8,128)} %get-tuple-element.19, f32[256,256]{1,0:T(8,128)} %get-tuple-element.17, f32[256,256]{1,0:T(8,128)S(1)} %copy-done), kind=kLoop, calls=%fused_computation | loop fusion | flops 262144 | bytes 1703936 | tf_op jit(solution)/shard_map/mul | solution.py:540
Async XLA Ops:
  65.7 119.3 %copy-start = (f32[256,256]{1,0:T(8,128)S(1)}, f32[256,256]{1,0:T(8,128)}, u32[]{:S(2)}) copy-start(f32[256,256]{1,0:T(8,128)} %get-tuple-element.18) | copy-start | bytes 786436

commit v10 on v9

--- a/solution.py
+++ b/solution.py
@@ -239,7 +239,8 @@
         pl.when(self.cond)(self.copy.wait)
 
 
-def spread_kernel(n_row, n_col, mid_ref, up_ref, down_ref, parts_ref, o_ref, sums_ref, up_bf, down_bf,
+def spread_kernel(n_row, n_col, scale, mid_ref, up_ref, down_ref, parts_ref, self_ref, o_ref, sums_ref, own,
+                  up_bf, down_bf,
                   from_down, from_up, ring_in, ring_out, far_in, far_out, far_from, up_send, down_send,
                   from_down_sem, from_up_sem, ring_send, ring_recv, far_send, far_recv, last_send, last_recv,
                   part, gath, rsend, rrecv, dsend, drecv, gsend, grecv):
@@ -299,8 +300,8 @@
         for step in range(1, n_col):
             value = local_total(step - 1)
             if step > 1:
-                value = value + ring_in[step - 2]
-            ring_out[step - 1] = value
+                value = value + ring_in[step - 2].astype(jnp.float32)
+            ring_out[step - 1] = value.astype(ring_out.dtype)
             copy = pltpu.make_async_remote_copy(
                 src_ref=ring_out.at[step - 1],
                 dst_ref=ring_in.at[step - 1],
@@ -311,7 +312,7 @@
             )
             copy.start()
             yield copy
-        o_ref[...] = local_total(n_col - 1) + ring_in[n_col - 2]
+        own[...] = local_total(n_col - 1) + ring_in[n_col - 2].astype(jnp.float32)
 
     def far_steps(side, part_ref, far):
         for step in range(1, n_col):
@@ -364,36 +365,35 @@
     pl.when(far_down)(lasts[0].wait_recv)
     pl.when(far_up)(lasts[1].wait_recv)
     zero = jnp.zeros(o_ref.shape, jnp.float32)
-    o_ref[...] = (
-        o_ref[...]
-        + jnp.where(far_down, far_from[0], zero)
-        + jnp.where(far_up, far_from[1], zero)
-    )
+    total = own[...] + jnp.where(far_down, far_from[0], zero) + jnp.where(far_up, far_from[1], zero)
+    o_ref[...] = (total + self_ref[...]).astype(o_ref.dtype)
+    sums_ref[...] = sums_ref[...] * scale
     for _, (to_up, to_down) in halos:
         pl.when(jnp.logical_not(far_up))(to_up.wait_send)
         pl.when(jnp.logical_not(far_down))(to_down.wait_send)
 
 
-def reduce_spread(mid, up_part, down_part, parts, n_row, n_col):
+def reduce_spread(mid, up_part, down_part, parts, self_feature, scale, n_row, n_col):
     _, rows, width = mid.shape
     col_bits = n_col.bit_length() - 1
     row_bits = n_row.bit_length() - 1
     stacked, _ = parts.shape
     return pl.pallas_call(
-        functools.partial(spread_kernel, n_row, n_col),
+        functools.partial(spread_kernel, n_row, n_col, scale),
         out_shape=(
-            jax.ShapeDtypeStruct((rows, width), jnp.float32),
+            jax.ShapeDtypeStruct((rows, width), jnp.bfloat16),
             jax.ShapeDtypeStruct(parts.shape, jnp.float32),
         ),
-        in_specs=[pl.BlockSpec(memory_space=pltpu.VMEM)] * 4,
+        in_specs=[pl.BlockSpec(memory_space=pltpu.VMEM)] * 5,
         out_specs=(pl.BlockSpec(memory_space=pltpu.VMEM),) * 2,
         scratch_shapes=[
+            pltpu.VMEM((rows, width), jnp.float32),
             pltpu.VMEM((n_col, rows, width), jnp.bfloat16),
             pltpu.VMEM((n_col, rows, width), jnp.bfloat16),
             pltpu.VMEM((n_col, rows, width), jnp.bfloat16),
             pltpu.VMEM((n_col, rows, width), jnp.bfloat16),
-            pltpu.VMEM((n_col - 1, rows, width), jnp.float32),
-            pltpu.VMEM((n_col - 1, rows, width), jnp.float32),
+            pltpu.VMEM((n_col - 1, rows, width), jnp.bfloat16),
+            pltpu.VMEM((n_col - 1, rows, width), jnp.bfloat16),
             pltpu.VMEM((2, n_col - 1, rows, width), jnp.float32),
             pltpu.VMEM((2, n_col, rows, width), jnp.float32),
             pltpu.VMEM((2, rows, width), jnp.float32),
@@ -417,7 +417,7 @@
             pltpu.SemaphoreType.DMA((n_col,)),
         ],
         compiler_params=pltpu.CompilerParams(collective_id=2, has_side_effects=True),
-    )(mid, up_part, down_part, parts)
+    )(mid, up_part, down_part, parts, self_feature)
 
 
 def local_kernel(rows_ref, cols_ref, count_ref, window_ref, tiles_ref, feat_ref, w_ref, ws_ref, cot_ref,
@@ -526,18 +526,19 @@
         weight_self,
         cotangent,
     )
-    own_share, summed_parts = reduce_spread(
+    factor = 1.0 / math.sqrt(node_rows * col_count * row_count)
+    feature_grad, summed_parts = reduce_spread(
         mid.reshape(col_count, node_rows, width),
         up_part.reshape(col_count, node_rows, width),
         down_part.reshape(col_count, node_rows, width),
         parts,
+        self_feature,
+        factor,
         row_count,
         col_count,
     )
-    feature_grad = (own_share + self_feature).astype(jnp.bfloat16)
     weight_total, self_total = summed_parts[:width], summed_parts[width:]
-    factor = 1.0 / math.sqrt(node_rows * col_count * row_count)
-    return (activations, feature_grad, weight_total * factor, self_total * factor)
+    return (activations, feature_grad, weight_total, self_total)
 
 
 def solution(mesh):

time: 187 us -> 178 us (0.952)
  Pallas kernels: 184 us -> 173 us
  local copies, waits for them, and re-layouts: 0.01 us -> 3.42 us
  other arithmetic: 1.96 us -> 0 us
    pallas_call x1, Pallas kernels: 119 us -> 103 us  [reduce_spread(): pl.pallas_call(functools.partial(spread_kernel, n_row, n_col, scale), out...]
    pallas_call x1, Pallas kernels: 6.78 us -> 11.7 us  [local_math(): pl.pallas_call(local_kernel, out_shape=(jax.ShapeDtypeStruct((nodes, widt...]
    mul x1 -> x0, other arithmetic: 1.96 us -> none  [shards(): self_total * factor]
where the time goes in v10:
time: 178 us; the launch traced here: 177 us
  Pallas kernels  173 us (97%)
  local copies, waits for them, and re-layouts  3.42 us (2%)
    pallas_call x1, Pallas kernels, reduce_spread(): pl.pallas_call(functools.partial(spread_kernel, n_row, n_col, scale), out...  103 us
    pallas_call x1, Pallas kernels, gather_window(): pl.pallas_call(functools.partial(gather_kernel, n_row, n_col), out_shape=...  57.7 us
    pallas_call x1, Pallas kernels, local_math(): pl.pallas_call(local_kernel, out_shape=(jax.ShapeDtypeStruct((nodes, widt...  11.7 us

profile of v10, /device:TPU:9, one launch (start us, length us, event | category | flops | bytes accessed | tf_op | source)
XLA Modules:
  0.0 177.3 jit_solution(16989969483662963277)
XLA Ops:
  1.3 57.7 %shard_map.111 = bf16[3,8,256,256]{3,2,1,0:T(8,128)(2,1)} custom-call(bf16[256,256]{1,0:T(8,128)(2,1)} %feat_ref.1), custom_call_target="tpu_custom_call" | custom-call | tf_op jit(solution)/shard_map/pallas_call | solution.py:217
  59.0 11.7 %shard_map.112 = (bf16[256,256]{1,0:T(8,128)(2,1)}, f32[512,256]{1,0:T(8,128)}, f32[256,256]{1,0:T(8,128)}, f32[16,128,256]{2,1,0:T(8,128)}, f32[16,128,256]{2,1,0:T(8,128)}, /*index=5*/f32[16,128,256]{2,1,0:T(8,128)}) custom-call(s32[32]{0:T(128)} %bitcast.14, s32[32]{0:T(128)} %bitcast.15, s32[1]{0:T(128)} %bitcast.8.count_ref, ...), custom_call_target="tpu_custom_call" | custom-call | tf_op jit(solution)/shard_map/pallas_call | solution.py:483
  70.7 103.2 %shard_map.113 = (bf16[256,256]{1,0:T(8,128)(2,1)}, f32[512,256]{1,0:T(8,128)}) custom-call(f32[8,256,256]{2,1,0:T(8,128)} %bitcast.10, f32[8,256,256]{2,1,0:T(8,128)} %bitcast.11, f32[8,256,256]{2,1,0:T(8,128)} %bitcast.12, f32[512,256]{1,0:T(8,128)} %get-tuple-element.16.parts_ref, f32[256,256]{1,0:T(8,128)} %get-tuple-element.17.self_ref), custom_call_target="tpu_custom_call" | custom-call | tf_op jit(solution)/shard_map/pallas_call | solution.py:381
  173.9 1.9 %fusion = (f32[256,256]{1,0:T(8,128)}, f32[256,256]{1,0:T(8,128)}) fusion(f32[512,256]{1,0:T(8,128)} %get-tuple-element.19), kind=kLoop, calls=%fused_computation | loop fusion | bytes 1048576 | tf_op jit(solution)/shard_map/slice | solution.py:540
  175.8 1.6 copy.14

commit v11 on v10

--- a/solution.py
+++ b/solution.py
@@ -137,7 +137,7 @@
     pred = ring_col((p + n_col - 1) % n_col, n_col)
     up = (row + 1) % n_row
     down = (row + n_row - 1) % n_row
-    half = max(n_row // 2, 1)
+    half = 8 if n_row % 8 == 0 else n_row
     far = {0: row % half == 0, 2: (row + 1) % half == 0}
     barrier = pltpu.get_barrier_semaphore()
     for device in ((row, succ), (row, pred), (up, col), (down, col)):
@@ -251,7 +251,7 @@
     pred = ring_col((p + n_col - 1) % n_col, n_col)
     up = (row + 1) % n_row
     down = (row + n_row - 1) % n_row
-    half = max(n_row // 2, 1)
+    half = 8 if n_row % 8 == 0 else n_row
     far_down = row % half == 0
     far_up = (row + 1) % half == 0
     partners = [(row, succ), (row, pred), (up, col), (down, col)]

time: 178 us -> 176 us (0.989)
  the two profiles are of different devices: /device:TPU:9 before, /device:TPU:57 now
where the time goes in v11:
time: 176 us; the launch traced here: 173 us
  Pallas kernels  169 us (96%)
  local copies, waits for them, and re-layouts  3.42 us (2%)
    pallas_call x1, Pallas kernels, reduce_spread(): pl.pallas_call(functools.partial(spread_kernel, n_row, n_col, scale), out...  107 us
    pallas_call x1, Pallas kernels, gather_window(): pl.pallas_call(functools.partial(gather_kernel, n_row, n_col), out_shape=...  54.2 us
    pallas_call x1, Pallas kernels, local_math(): pl.pallas_call(local_kernel, out_shape=(jax.ShapeDtypeStruct((nodes, widt...  7.84 us

profile of v11, /device:TPU:57, one launch (start us, length us, event | category | flops | bytes accessed | tf_op | source)
XLA Modules:
  0.0 173.4 jit_solution(6765952745630833100)
XLA Ops:
  1.3 54.2 %shard_map.111 = bf16[3,8,256,256]{3,2,1,0:T(8,128)(2,1)} custom-call(bf16[256,256]{1,0:T(8,128)(2,1)} %feat_ref.1), custom_call_target="tpu_custom_call" | custom-call | tf_op jit(solution)/shard_map/pallas_call | solution.py:217
  55.5 7.8 %shard_map.112 = (bf16[256,256]{1,0:T(8,128)(2,1)}, f32[512,256]{1,0:T(8,128)}, f32[256,256]{1,0:T(8,128)}, f32[16,128,256]{2,1,0:T(8,128)}, f32[16,128,256]{2,1,0:T(8,128)}, /*index=5*/f32[16,128,256]{2,1,0:T(8,128)}) custom-call(s32[32]{0:T(128)} %bitcast.14, s32[32]{0:T(128)} %bitcast.15, s32[1]{0:T(128)} %bitcast.8.count_ref, ...), custom_call_target="tpu_custom_call" | custom-call | tf_op jit(solution)/shard_map/pallas_call | solution.py:483
  63.3 106.7 %shard_map.113 = (bf16[256,256]{1,0:T(8,128)(2,1)}, f32[512,256]{1,0:T(8,128)}) custom-call(f32[8,256,256]{2,1,0:T(8,128)} %bitcast.10, f32[8,256,256]{2,1,0:T(8,128)} %bitcast.11, f32[8,256,256]{2,1,0:T(8,128)} %bitcast.12, f32[512,256]{1,0:T(8,128)} %get-tuple-element.16.parts_ref, f32[256,256]{1,0:T(8,128)} %get-tuple-element.17.self_ref), custom_call_target="tpu_custom_call" | custom-call | tf_op jit(solution)/shard_map/pallas_call | solution.py:381
  170.0 1.9 %fusion = (f32[256,256]{1,0:T(8,128)}, f32[256,256]{1,0:T(8,128)}) fusion(f32[512,256]{1,0:T(8,128)} %get-tuple-element.19), kind=kLoop, calls=%fused_computation | loop fusion | bytes 1048576 | tf_op jit(solution)/shard_map/slice | solution.py:540
  171.9 1.6 copy.14

commit v12 on v10

--- a/solution.py
+++ b/solution.py
@@ -266,6 +266,8 @@
     up_bf[...] = up_ref[...].astype(up_bf.dtype)
     down_bf[...] = down_ref[...].astype(down_bf.dtype)
     halos = []
+    starts = []
+    lead = 2
     for step in range(1, n_col + 1):
         block = ring_col((p - step + 2 * n_col) % n_col, n_col)
         pair = []
@@ -281,9 +283,17 @@
                 device_id=(target, col),
                 device_id_type=MESH,
             )
-            pl.when(jnp.logical_not(far))(copy.start)
-            pair.append(copy)
-        halos.append((block, pair))
+            pair.append((copy, far))
+        halos.append((block, [copy for copy, _ in pair]))
+        starts.append(pair)
+
+    def start_halo(index):
+        if index < len(starts):
+            for copy, far in starts[index]:
+                pl.when(jnp.logical_not(far))(copy.start)
+
+    for index in range(lead):
+        start_halo(index)
 
     def local_total(index):
         block, (from_below, from_above) = halos[index]
@@ -298,6 +308,7 @@
 
     def ring_steps():
         for step in range(1, n_col):
+            start_halo(step - 1 + lead)
             value = local_total(step - 1)
             if step > 1:
                 value = value + ring_in[step - 2].astype(jnp.float32)
@@ -312,6 +323,7 @@
             )
             copy.start()
             yield copy
+        start_halo(n_col - 1 + lead)
         own[...] = local_total(n_col - 1) + ring_in[n_col - 2].astype(jnp.float32)
 
     def far_steps(side, part_ref, far):

time: 178 us -> 176 us (0.989)
  the two profiles are of different devices: /device:TPU:9 before, /device:TPU:8 now
where the time goes in v12:
time: 176 us
  Pallas kernels  171 us (97%)
  local copies, waits for them, and re-layouts  3.42 us (2%)
    pallas_call x1, Pallas kernels, reduce_spread(): pl.pallas_call(functools.partial(spread_kernel, n_row, n_col, scale), out...  105 us
    pallas_call x1, Pallas kernels, gather_window(): pl.pallas_call(functools.partial(gather_kernel, n_row, n_col), out_shape=...  56 us
    pallas_call x1, Pallas kernels, local_math(): pl.pallas_call(local_kernel, out_shape=(jax.ShapeDtypeStruct((nodes, widt...  10.3 us

profile of v12, /device:TPU:8, one launch (start us, length us, event | category | flops | bytes accessed | tf_op | source)
XLA Modules:
  0.0 175.6 jit_solution(10494282725054958883)
XLA Ops:
  1.3 56.0 %shard_map.111 = bf16[3,8,256,256]{3,2,1,0:T(8,128)(2,1)} custom-call(bf16[256,256]{1,0:T(8,128)(2,1)} %feat_ref.1), custom_call_target="tpu_custom_call" | custom-call | tf_op jit(solution)/shard_map/pallas_call | solution.py:217
  57.3 10.3 %shard_map.112 = (bf16[256,256]{1,0:T(8,128)(2,1)}, f32[512,256]{1,0:T(8,128)}, f32[256,256]{1,0:T(8,128)}, f32[16,128,256]{2,1,0:T(8,128)}, f32[16,128,256]{2,1,0:T(8,128)}, /*index=5*/f32[16,128,256]{2,1,0:T(8,128)}) custom-call(s32[32]{0:T(128)} %bitcast.14, s32[32]{0:T(128)} %bitcast.15, s32[1]{0:T(128)} %bitcast.8.count_ref, ...), custom_call_target="tpu_custom_call" | custom-call | tf_op jit(solution)/shard_map/pallas_call | solution.py:495
  67.6 104.5 %shard_map.113 = (bf16[256,256]{1,0:T(8,128)(2,1)}, f32[512,256]{1,0:T(8,128)}) custom-call(f32[8,256,256]{2,1,0:T(8,128)} %bitcast.10, f32[8,256,256]{2,1,0:T(8,128)} %bitcast.11, f32[8,256,256]{2,1,0:T(8,128)} %bitcast.12, f32[512,256]{1,0:T(8,128)} %get-tuple-element.16.parts_ref, f32[256,256]{1,0:T(8,128)} %get-tuple-element.17.self_ref), custom_call_target="tpu_custom_call" | custom-call | tf_op jit(solution)/shard_map/pallas_call | solution.py:393
  172.1 1.9 %fusion = (f32[256,256]{1,0:T(8,128)}, f32[256,256]{1,0:T(8,128)}) fusion(f32[512,256]{1,0:T(8,128)} %get-tuple-element.19), kind=kLoop, calls=%fused_computation | loop fusion | bytes 1048576 | tf_op jit(solution)/shard_map/slice | solution.py:552
  174.0 1.6 copy.14

commit v13 on v12

--- a/solution.py
+++ b/solution.py
@@ -239,7 +239,7 @@
         pl.when(self.cond)(self.copy.wait)
 
 
-def spread_kernel(n_row, n_col, scale, mid_ref, up_ref, down_ref, parts_ref, self_ref, o_ref, sums_ref, own,
+def spread_kernel(n_row, n_col, scale, spread_ref, parts_ref, self_ref, o_ref, sums_ref, own,
                   up_bf, down_bf,
                   from_down, from_up, ring_in, ring_out, far_in, far_out, far_from, up_send, down_send,
                   from_down_sem, from_up_sem, ring_send, ring_recv, far_send, far_recv, last_send, last_recv,
@@ -263,6 +263,7 @@
 
         pl.when(jnp.logical_or(device[0] != row, device[1] != col))(signal)
     pl.semaphore_wait(barrier, len(partners) - 1)
+    mid_ref, up_ref, down_ref = spread_ref.at[1], spread_ref.at[2], spread_ref.at[0]
     up_bf[...] = up_ref[...].astype(up_bf.dtype)
     down_bf[...] = down_ref[...].astype(down_bf.dtype)
     halos = []
@@ -385,8 +386,8 @@
         pl.when(jnp.logical_not(far_down))(to_down.wait_send)
 
 
-def reduce_spread(mid, up_part, down_part, parts, self_feature, scale, n_row, n_col):
-    _, rows, width = mid.shape
+def reduce_spread(spread, parts, self_feature, scale, n_row, n_col):
+    _, _, rows, width = spread.shape
     col_bits = n_col.bit_length() - 1
     row_bits = n_row.bit_length() - 1
     stacked, _ = parts.shape
@@ -396,7 +397,7 @@
             jax.ShapeDtypeStruct((rows, width), jnp.bfloat16),
             jax.ShapeDtypeStruct(parts.shape, jnp.float32),
         ),
-        in_specs=[pl.BlockSpec(memory_space=pltpu.VMEM)] * 5,
+        in_specs=[pl.BlockSpec(memory_space=pltpu.VMEM)] * 3,
         out_specs=(pl.BlockSpec(memory_space=pltpu.VMEM),) * 2,
         scratch_shapes=[
             pltpu.VMEM((rows, width), jnp.float32),
@@ -429,14 +430,13 @@
             pltpu.SemaphoreType.DMA((n_col,)),
         ],
         compiler_params=pltpu.CompilerParams(collective_id=2, has_side_effects=True),
-    )(mid, up_part, down_part, parts, self_feature)
+    )(spread, parts, self_feature)
 
 
 def local_kernel(rows_ref, cols_ref, count_ref, window_ref, tiles_ref, feat_ref, w_ref, ws_ref, cot_ref,
-                 act_ref, parts_ref, self_ref, mid_ref, up_ref, down_ref, acc, grad_agg, spread):
+                 act_ref, parts_ref, self_ref, spread, acc, grad_agg):
     tile = tiles_ref.shape[-1]
     nodes = acc.shape[0]
-    span = mid_ref.shape[0]
     count = jnp.minimum(count_ref[0], tiles_ref.shape[0])
     acc[...] = jnp.zeros_like(acc)
 
@@ -481,9 +481,6 @@
         return carry
 
     lax.fori_loop(0, count, backward, 0)
-    mid_ref[...] = spread[pl.ds(span, span)]
-    up_ref[...] = spread[pl.ds(2 * span, span)].astype(up_ref.dtype)
-    down_ref[...] = spread[pl.ds(0, span)].astype(down_ref.dtype)
 
 
 def local_math(slot_rows, slot_cols, count, window, tiles, features, weight, weight_self, cotangent):
@@ -498,16 +495,13 @@
             jax.ShapeDtypeStruct((nodes, width), jnp.bfloat16),
             jax.ShapeDtypeStruct((2 * width, width), jnp.float32),
             jax.ShapeDtypeStruct((nodes, width), jnp.float32),
-            jax.ShapeDtypeStruct((span, tile, width), jnp.float32),
-            jax.ShapeDtypeStruct((span, tile, width), jnp.float32),
-            jax.ShapeDtypeStruct((span, tile, width), jnp.float32),
+            jax.ShapeDtypeStruct((3 * span, tile, width), jnp.float32),
         ),
         in_specs=[smem, smem, smem] + [vmem] * 6,
-        out_specs=(vmem,) * 6,
+        out_specs=(vmem,) * 4,
         scratch_shapes=[
             pltpu.VMEM((nodes, width), jnp.float32),
             pltpu.VMEM((nodes, width), jnp.bfloat16),
-            pltpu.VMEM((3 * span, tile, width), jnp.float32),
         ],
     )(slot_rows, slot_cols, count, window, tiles, features, weight, weight_self, cotangent)
 
@@ -527,7 +521,7 @@
     span = col_count * per_block
     window = gather_window(features, row_count, col_count)
     window_tiles = window.reshape(-1, tile_side, width)
-    activations, parts, self_feature, mid, up_part, down_part = local_math(
+    activations, parts, self_feature, spread = local_math(
         slot_rows,
         slot_cols,
         tile_count[0],
@@ -540,9 +534,7 @@
     )
     factor = 1.0 / math.sqrt(node_rows * col_count * row_count)
     feature_grad, summed_parts = reduce_spread(
-        mid.reshape(col_count, node_rows, width),
-        up_part.reshape(col_count, node_rows, width),
-        down_part.reshape(col_count, node_rows, width),
+        spread.reshape(3, col_count, node_rows, width),
         parts,
         self_feature,
         factor,

time: 176 us -> 174 us (0.989)
  the two profiles are of different devices: /device:TPU:8 before, /device:TPU:25 now
where the time goes in v13:
time: 174 us; the launch traced here: 173 us
  Pallas kernels  168 us (97%)
  local copies, waits for them, and re-layouts  3.42 us (2%)
    pallas_call x1, Pallas kernels, reduce_spread(): pl.pallas_call(functools.partial(spread_kernel, n_row, n_col, scale), out...  99.3 us
    pallas_call x1, Pallas kernels, gather_window(): pl.pallas_call(functools.partial(gather_kernel, n_row, n_col), out_shape=...  55.6 us
    pallas_call x1, Pallas kernels, local_math(): pl.pallas_call(local_kernel, out_shape=(jax.ShapeDtypeStruct((nodes, widt...  12.9 us

profile of v13, /device:TPU:25, one launch (start us, length us, event | category | flops | bytes accessed | tf_op | source)
XLA Modules:
  0.0 172.6 jit_solution(5069127906565792942)
XLA Ops:
  1.3 55.6 %shard_map.111 = bf16[3,8,256,256]{3,2,1,0:T(8,128)(2,1)} custom-call(bf16[256,256]{1,0:T(8,128)(2,1)} %feat_ref.1), custom_call_target="tpu_custom_call" | custom-call | tf_op jit(solution)/shard_map/pallas_call | solution.py:217
  56.9 12.9 %shard_map.112 = (bf16[256,256]{1,0:T(8,128)(2,1)}, f32[512,256]{1,0:T(8,128)}, f32[256,256]{1,0:T(8,128)}, f32[48,128,256]{2,1,0:T(8,128)}) custom-call(s32[32]{0:T(128)} %bitcast.10, s32[32]{0:T(128)} %bitcast.11, s32[1]{0:T(128)} %bitcast.6.count_ref, bf16[48,128,256]{2,1,0:T(8,128)(2,1)} %bitcast.7, bf16[32,128,128]{2,1,0:T(8,128)(2,1)} %bitcast.9, ...), custom_call_target="tpu_custom_call" | custom-call | tf_op jit(solution)/shard_map/pallas_call | solution.py:492
  69.9 99.3 %shard_map.113 = (bf16[256,256]{1,0:T(8,128)(2,1)}, f32[512,256]{1,0:T(8,128)}) custom-call(f32[3,8,256,256]{3,2,1,0:T(8,128)} %bitcast.8, f32[512,256]{1,0:T(8,128)} %get-tuple-element.12.parts_ref, f32[256,256]{1,0:T(8,128)} %get-tuple-element.13.self_ref), custom_call_target="tpu_custom_call" | custom-call | tf_op jit(solution)/shard_map/pallas_call | solution.py:394
  169.2 1.9 %fusion = (f32[256,256]{1,0:T(8,128)}, f32[256,256]{1,0:T(8,128)}) fusion(f32[512,256]{1,0:T(8,128)} %get-tuple-element.15), kind=kLoop, calls=%fused_computation | loop fusion | bytes 1048576 | tf_op jit(solution)/shard_map/slice | solution.py:544
  171.0 1.6 copy.14

commit v14 on v13

--- a/solution.py
+++ b/solution.py
@@ -163,6 +163,7 @@
     for copy in halos[0][1].values():
         copy.start()
     sent = col
+    pending = []
     for step in range(1, n_col):
         copies = {}
         for group in (1, 0, 2):
@@ -182,11 +183,11 @@
                 if step == 1:
                     halos[0][1][group].wait_recv()
                 copies[group].start()
-        copies[1].wait()
+        copies[1].wait_recv()
+        pending.append((copies[1], None))
         for group in (0, 2):
-            @pl.when(far[group])
-            def _():
-                copies[group].wait()
+            pl.when(far[group])(copies[group].wait_recv)
+            pending.append((copies[group], far[group]))
         sent = ring_col((p - step + n_col) % n_col, n_col)
         forward = halo(w_ref.at[1, sent], sent, step)
         halos.append((sent, forward))
@@ -194,6 +195,11 @@
             @pl.when(jnp.logical_not(far[2 - slot]))
             def _():
                 forward[slot].start()
+    for copy, cond in pending:
+        if cond is None:
+            copy.wait_send()
+        else:
+            pl.when(cond)(copy.wait_send)
     for copy in halos[0][1].values():
         copy.wait_send()
     for slot in (0, 2):
@@ -231,12 +237,17 @@
 
 
 class Gated:
-    def __init__(self, copy, cond):
+    def __init__(self, copy, cond, pending):
         self.copy = copy
         self.cond = cond
+        self.pending = pending
 
     def wait(self):
-        pl.when(self.cond)(self.copy.wait)
+        pl.when(self.cond)(self.copy.wait_recv)
+        self.pending.append(self)
+
+    def finish(self):
+        pl.when(self.cond)(self.copy.wait_send)
 
 
 def spread_kernel(n_row, n_col, scale, spread_ref, parts_ref, self_ref, o_ref, sums_ref, own,
@@ -323,7 +334,7 @@
                 device_id_type=MESH,
             )
             copy.start()
-            yield copy
+            yield Gated(copy, True, pending)
         start_halo(n_col - 1 + lead)
         own[...] = local_total(n_col - 1) + ring_in[n_col - 2].astype(jnp.float32)
 
@@ -347,13 +358,14 @@
                 copy.start()
 
             pl.when(far)(send)
-            yield Gated(copy, far)
+            yield Gated(copy, far, pending)
 
         def finish():
             far_out[side, n_col - 1] = part_ref[col] + far_in[side, n_col - 2]
 
         pl.when(far)(finish)
 
+    pending = []
     run_together(
         allreduce_steps(n_row, n_col, row, col, parts_ref, sums_ref, part, gath,
                         rsend, rrecv, dsend, drecv, gsend, grecv),
@@ -361,6 +373,8 @@
         far_steps(0, up_ref, far_up),
         far_steps(1, down_ref, far_down),
     )
+    for item in pending:
+        item.finish()
     lasts = []
     for side, target, slot, far in ((0, up, 0, far_up), (1, down, 1, far_down)):
         copy = pltpu.make_async_remote_copy(

time: 174 us -> 167 us (0.960)
  the two profiles are of different devices: /device:TPU:25 before, /device:TPU:57 now
where the time goes in v14:
time: 167 us; the launch traced here: 164 us
  Pallas kernels  160 us (96%)
  local copies, waits for them, and re-layouts  3.42 us (2%)
    pallas_call x1, Pallas kernels, reduce_spread(): pl.pallas_call(functools.partial(spread_kernel, n_row, n_col, scale), out...  98.6 us
    pallas_call x1, Pallas kernels, gather_window(): pl.pallas_call(functools.partial(gather_kernel, n_row, n_col), out_shape=...  54.2 us
    pallas_call x1, Pallas kernels, local_math(): pl.pallas_call(local_kernel, out_shape=(jax.ShapeDtypeStruct((nodes, widt...  6.96 us

profile of v14, /device:TPU:57, one launch (start us, length us, event | category | flops | bytes accessed | tf_op | source)
XLA Modules:
  0.0 164.5 jit_solution(14997524448203721998)
XLA Ops:
  1.3 54.2 %shard_map.111 = bf16[3,8,256,256]{3,2,1,0:T(8,128)(2,1)} custom-call(bf16[256,256]{1,0:T(8,128)(2,1)} %feat_ref.1), custom_call_target="tpu_custom_call" | custom-call | tf_op jit(solution)/shard_map/pallas_call | solution.py:223
  55.5 7.0 %shard_map.112 = (bf16[256,256]{1,0:T(8,128)(2,1)}, f32[512,256]{1,0:T(8,128)}, f32[256,256]{1,0:T(8,128)}, f32[48,128,256]{2,1,0:T(8,128)}) custom-call(s32[32]{0:T(128)} %bitcast.10, s32[32]{0:T(128)} %bitcast.11, s32[1]{0:T(128)} %bitcast.6.count_ref, bf16[48,128,256]{2,1,0:T(8,128)(2,1)} %bitcast.7, bf16[32,128,128]{2,1,0:T(8,128)(2,1)} %bitcast.9, ...), custom_call_target="tpu_custom_call" | custom-call | tf_op jit(solution)/shard_map/pallas_call | solution.py:506
  62.5 98.6 %shard_map.113 = (bf16[256,256]{1,0:T(8,128)(2,1)}, f32[512,256]{1,0:T(8,128)}) custom-call(f32[3,8,256,256]{3,2,1,0:T(8,128)} %bitcast.8, f32[512,256]{1,0:T(8,128)} %get-tuple-element.12.parts_ref, f32[256,256]{1,0:T(8,128)} %get-tuple-element.13.self_ref), custom_call_target="tpu_custom_call" | custom-call | tf_op jit(solution)/shard_map/pallas_call | solution.py:408
  161.1 1.9 %fusion = (f32[256,256]{1,0:T(8,128)}, f32[256,256]{1,0:T(8,128)}) fusion(f32[512,256]{1,0:T(8,128)} %get-tuple-element.15), kind=kLoop, calls=%fused_computation | loop fusion | bytes 1048576 | tf_op jit(solution)/shard_map/slice | solution.py:558
  162.9 1.6 copy.14

commit v15 on v13

--- a/solution.py
+++ b/solution.py
@@ -268,7 +268,7 @@
     down_bf[...] = down_ref[...].astype(down_bf.dtype)
     halos = []
     starts = []
-    lead = 2
+    lead = 3
     for step in range(1, n_col + 1):
         block = ring_col((p - step + 2 * n_col) % n_col, n_col)
         pair = []

time: 174 us -> 173 us (level)
  the two profiles are of different devices: /device:TPU:25 before, /device:TPU:57 now
where the time goes in v15:
time: 173 us; the launch traced here: 172 us
  Pallas kernels  167 us (97%)
  local copies, waits for them, and re-layouts  3.42 us (2%)
    pallas_call x1, Pallas kernels, reduce_spread(): pl.pallas_call(functools.partial(spread_kernel, n_row, n_col, scale), out...  102 us
    pallas_call x1, Pallas kernels, gather_window(): pl.pallas_call(functools.partial(gather_kernel, n_row, n_col), out_shape=...  54.2 us
    pallas_call x1, Pallas kernels, local_math(): pl.pallas_call(local_kernel, out_shape=(jax.ShapeDtypeStruct((nodes, widt...  10.1 us

profile of v15, /device:TPU:57, one launch (start us, length us, event | category | flops | bytes accessed | tf_op | source)
XLA Modules:
  0.0 171.5 jit_solution(5559746576839868381)
XLA Ops:
  1.3 54.2 %shard_map.111 = bf16[3,8,256,256]{3,2,1,0:T(8,128)(2,1)} custom-call(bf16[256,256]{1,0:T(8,128)(2,1)} %feat_ref.1), custom_call_target="tpu_custom_call" | custom-call | tf_op jit(solution)/shard_map/pallas_call | solution.py:217
  55.5 10.1 %shard_map.112 = (bf16[256,256]{1,0:T(8,128)(2,1)}, f32[512,256]{1,0:T(8,128)}, f32[256,256]{1,0:T(8,128)}, f32[48,128,256]{2,1,0:T(8,128)}) custom-call(s32[32]{0:T(128)} %bitcast.10, s32[32]{0:T(128)} %bitcast.11, s32[1]{0:T(128)} %bitcast.6.count_ref, bf16[48,128,256]{2,1,0:T(8,128)(2,1)} %bitcast.7, bf16[32,128,128]{2,1,0:T(8,128)(2,1)} %bitcast.9, ...), custom_call_target="tpu_custom_call" | custom-call | tf_op jit(solution)/shard_map/pallas_call | solution.py:492
  65.6 102.5 %shard_map.113 = (bf16[256,256]{1,0:T(8,128)(2,1)}, f32[512,256]{1,0:T(8,128)}) custom-call(f32[3,8,256,256]{3,2,1,0:T(8,128)} %bitcast.8, f32[512,256]{1,0:T(8,128)} %get-tuple-element.12.parts_ref, f32[256,256]{1,0:T(8,128)} %get-tuple-element.13.self_ref), custom_call_target="tpu_custom_call" | custom-call | tf_op jit(solution)/shard_map/pallas_call | solution.py:394
  168.1 1.9 %fusion = (f32[256,256]{1,0:T(8,128)}, f32[256,256]{1,0:T(8,128)}) fusion(f32[512,256]{1,0:T(8,128)} %get-tuple-element.15), kind=kLoop, calls=%fused_computation | loop fusion | bytes 1048576 | tf_op jit(solution)/shard_map/slice | solution.py:544
  170.0 1.6 copy.14

commit v16 on v15

--- a/solution.py
+++ b/solution.py
@@ -268,7 +268,7 @@
     down_bf[...] = down_ref[...].astype(down_bf.dtype)
     halos = []
     starts = []
-    lead = 3
+    lead = 1
     for step in range(1, n_col + 1):
         block = ring_col((p - step + 2 * n_col) % n_col, n_col)
         pair = []

time: 173 us -> 171 us (0.988)
    pallas_call x1, Pallas kernels: 10.1 us -> 6.61 us  [local_math(): pl.pallas_call(local_kernel, out_shape=(jax.ShapeDtypeStruct((nodes, widt...]
    pallas_call x1, Pallas kernels: 102 us -> 105 us  [reduce_spread(): pl.pallas_call(functools.partial(spread_kernel, n_row, n_col, scale), out...]
where the time goes in v16:
time: 171 us
  Pallas kernels  166 us (97%)
  local copies, waits for them, and re-layouts  3.42 us (2%)
    pallas_call x1, Pallas kernels, reduce_spread(): pl.pallas_call(functools.partial(spread_kernel, n_row, n_col, scale), out...  105 us
    pallas_call x1, Pallas kernels, gather_window(): pl.pallas_call(functools.partial(gather_kernel, n_row, n_col), out_shape=...  54.2 us
    pallas_call x1, Pallas kernels, local_math(): pl.pallas_call(local_kernel, out_shape=(jax.ShapeDtypeStruct((nodes, widt...  6.61 us

profile of v16, /device:TPU:57, one launch (start us, length us, event | category | flops | bytes accessed | tf_op | source)
XLA Modules:
  0.0 170.8 jit_solution(9636821402945951940)
XLA Ops:
  1.3 54.2 %shard_map.111 = bf16[3,8,256,256]{3,2,1,0:T(8,128)(2,1)} custom-call(bf16[256,256]{1,0:T(8,128)(2,1)} %feat_ref.1), custom_call_target="tpu_custom_call" | custom-call | tf_op jit(solution)/shard_map/pallas_call | solution.py:217
  55.5 6.6 %shard_map.112 = (bf16[256,256]{1,0:T(8,128)(2,1)}, f32[512,256]{1,0:T(8,128)}, f32[256,256]{1,0:T(8,128)}, f32[48,128,256]{2,1,0:T(8,128)}) custom-call(s32[32]{0:T(128)} %bitcast.10, s32[32]{0:T(128)} %bitcast.11, s32[1]{0:T(128)} %bitcast.6.count_ref, bf16[48,128,256]{2,1,0:T(8,128)(2,1)} %bitcast.7, bf16[32,128,128]{2,1,0:T(8,128)(2,1)} %bitcast.9, ...), custom_call_target="tpu_custom_call" | custom-call | tf_op jit(solution)/shard_map/pallas_call | solution.py:492
  62.1 105.3 %shard_map.113 = (bf16[256,256]{1,0:T(8,128)(2,1)}, f32[512,256]{1,0:T(8,128)}) custom-call(f32[3,8,256,256]{3,2,1,0:T(8,128)} %bitcast.8, f32[512,256]{1,0:T(8,128)} %get-tuple-element.12.parts_ref, f32[256,256]{1,0:T(8,128)} %get-tuple-element.13.self_ref), custom_call_target="tpu_custom_call" | custom-call | tf_op jit(solution)/shard_map/pallas_call | solution.py:394
  167.4 1.9 %fusion = (f32[256,256]{1,0:T(8,128)}, f32[256,256]{1,0:T(8,128)}) fusion(f32[512,256]{1,0:T(8,128)} %get-tuple-element.15), kind=kLoop, calls=%fused_computation | loop fusion | bytes 1048576 | tf_op jit(solution)/shard_map/slice | solution.py:544
  169.3 1.6 copy.14

commit v17 on v13

--- a/solution.py
+++ b/solution.py
@@ -162,7 +162,12 @@
     halos = [(col, halo(x_ref, col, 0))]
     for copy in halos[0][1].values():
         copy.start()
+    def start_forward(forward):
+        for slot in (0, 2):
+            pl.when(jnp.logical_not(far[2 - slot]))(forward[slot].start)
+
     sent = col
+    deferred = None
     for step in range(1, n_col):
         copies = {}
         for group in (1, 0, 2):
@@ -182,18 +187,17 @@
                 if step == 1:
                     halos[0][1][group].wait_recv()
                 copies[group].start()
+        if deferred is not None:
+            start_forward(deferred)
         copies[1].wait()
         for group in (0, 2):
             @pl.when(far[group])
             def _():
                 copies[group].wait()
         sent = ring_col((p - step + n_col) % n_col, n_col)
-        forward = halo(w_ref.at[1, sent], sent, step)
-        halos.append((sent, forward))
-        for slot in (0, 2):
-            @pl.when(jnp.logical_not(far[2 - slot]))
-            def _():
-                forward[slot].start()
+        deferred = halo(w_ref.at[1, sent], sent, step)
+        halos.append((sent, deferred))
+    start_forward(deferred)
     for copy in halos[0][1].values():
         copy.wait_send()
     for slot in (0, 2):

time: 174 us -> 176 us (1.011)
  the two profiles are of different devices: /device:TPU:25 before, /device:TPU:57 now
where the time goes in v17:
time: 176 us; the launch traced here: 175 us
  Pallas kernels  171 us (97%)
  local copies, waits for them, and re-layouts  3.42 us (2%)
    pallas_call x1, Pallas kernels, reduce_spread(): pl.pallas_call(functools.partial(spread_kernel, n_row, n_col, scale), out...  110 us
    pallas_call x1, Pallas kernels, gather_window(): pl.pallas_call(functools.partial(gather_kernel, n_row, n_col), out_shape=...  54.2 us
    pallas_call x1, Pallas kernels, local_math(): pl.pallas_call(local_kernel, out_shape=(jax.ShapeDtypeStruct((nodes, widt...  6.61 us

profile of v17, /device:TPU:57, one launch (start us, length us, event | category | flops | bytes accessed | tf_op | source)
XLA Modules:
  0.0 175.3 jit_solution(5477185920588576601)
XLA Ops:
  1.3 54.2 %shard_map.111 = bf16[3,8,256,256]{3,2,1,0:T(8,128)(2,1)} custom-call(bf16[256,256]{1,0:T(8,128)(2,1)} %feat_ref.1), custom_call_target="tpu_custom_call" | custom-call | tf_op jit(solution)/shard_map/pallas_call | solution.py:221
  55.5 6.6 %shard_map.112 = (bf16[256,256]{1,0:T(8,128)(2,1)}, f32[512,256]{1,0:T(8,128)}, f32[256,256]{1,0:T(8,128)}, f32[48,128,256]{2,1,0:T(8,128)}) custom-call(s32[32]{0:T(128)} %bitcast.10, s32[32]{0:T(128)} %bitcast.11, s32[1]{0:T(128)} %bitcast.6.count_ref, bf16[48,128,256]{2,1,0:T(8,128)(2,1)} %bitcast.7, bf16[32,128,128]{2,1,0:T(8,128)(2,1)} %bitcast.9, ...), custom_call_target="tpu_custom_call" | custom-call | tf_op jit(solution)/shard_map/pallas_call | solution.py:496
  62.1 109.8 %shard_map.113 = (bf16[256,256]{1,0:T(8,128)(2,1)}, f32[512,256]{1,0:T(8,128)}) custom-call(f32[3,8,256,256]{3,2,1,0:T(8,128)} %bitcast.8, f32[512,256]{1,0:T(8,128)} %get-tuple-element.12.parts_ref, f32[256,256]{1,0:T(8,128)} %get-tuple-element.13.self_ref), custom_call_target="tpu_custom_call" | custom-call | tf_op jit(solution)/shard_map/pallas_call | solution.py:398
  171.9 1.9 %fusion = (f32[256,256]{1,0:T(8,128)}, f32[256,256]{1,0:T(8,128)}) fusion(f32[512,256]{1,0:T(8,128)} %get-tuple-element.15), kind=kLoop, calls=%fused_computation | loop fusion | bytes 1048576 | tf_op jit(solution)/shard_map/slice | solution.py:548
  173.7 1.6 copy.14

commit v18 on v13

--- a/solution.py
+++ b/solution.py
@@ -239,7 +239,7 @@
         pl.when(self.cond)(self.copy.wait)
 
 
-def spread_kernel(n_row, n_col, scale, spread_ref, parts_ref, self_ref, o_ref, sums_ref, own,
+def spread_kernel(n_row, n_col, spread_ref, parts_ref, o_ref, sums_ref, own,
                   up_bf, down_bf,
                   from_down, from_up, ring_in, ring_out, far_in, far_out, far_from, up_send, down_send,
                   from_down_sem, from_up_sem, ring_send, ring_recv, far_send, far_recv, last_send, last_recv,
@@ -379,25 +379,24 @@
     pl.when(far_up)(lasts[1].wait_recv)
     zero = jnp.zeros(o_ref.shape, jnp.float32)
     total = own[...] + jnp.where(far_down, far_from[0], zero) + jnp.where(far_up, far_from[1], zero)
-    o_ref[...] = (total + self_ref[...]).astype(o_ref.dtype)
-    sums_ref[...] = sums_ref[...] * scale
+    o_ref[...] = total
     for _, (to_up, to_down) in halos:
         pl.when(jnp.logical_not(far_up))(to_up.wait_send)
         pl.when(jnp.logical_not(far_down))(to_down.wait_send)
 
 
-def reduce_spread(spread, parts, self_feature, scale, n_row, n_col):
+def reduce_spread(spread, parts, n_row, n_col):
     _, _, rows, width = spread.shape
     col_bits = n_col.bit_length() - 1
     row_bits = n_row.bit_length() - 1
     stacked, _ = parts.shape
     return pl.pallas_call(
-        functools.partial(spread_kernel, n_row, n_col, scale),
+        functools.partial(spread_kernel, n_row, n_col),
         out_shape=(
-            jax.ShapeDtypeStruct((rows, width), jnp.bfloat16),
+            jax.ShapeDtypeStruct((rows, width), jnp.float32),
             jax.ShapeDtypeStruct(parts.shape, jnp.float32),
         ),
-        in_specs=[pl.BlockSpec(memory_space=pltpu.VMEM)] * 3,
+        in_specs=[pl.BlockSpec(memory_space=pltpu.VMEM)] * 2,
         out_specs=(pl.BlockSpec(memory_space=pltpu.VMEM),) * 2,
         scratch_shapes=[
             pltpu.VMEM((rows, width), jnp.float32),
@@ -430,7 +429,7 @@
             pltpu.SemaphoreType.DMA((n_col,)),
         ],
         compiler_params=pltpu.CompilerParams(collective_id=2, has_side_effects=True),
-    )(spread, parts, self_feature)
+    )(spread, parts)
 
 
 def local_kernel(rows_ref, cols_ref, count_ref, window_ref, tiles_ref, feat_ref, w_ref, ws_ref, cot_ref,
@@ -533,16 +532,15 @@
         cotangent,
     )
     factor = 1.0 / math.sqrt(node_rows * col_count * row_count)
-    feature_grad, summed_parts = reduce_spread(
+    own_share, summed_parts = reduce_spread(
         spread.reshape(3, col_count, node_rows, width),
         parts,
-        self_feature,
-        factor,
         row_count,
         col_count,
     )
+    feature_grad = (own_share + self_feature).astype(jnp.bfloat16)
     weight_total, self_total = summed_parts[:width], summed_parts[width:]
-    return (activations, feature_grad, weight_total, self_total)
+    return (activations, feature_grad, weight_total * factor, self_total * factor)
 
 
 def solution(mesh):

time: 174 us -> 172 us (0.989)
  the two profiles are of different devices: /device:TPU:25 before, /device:TPU:57 now
where the time goes in v18:
time: 172 us; the launch traced here: 170 us
  Pallas kernels  167 us (97%)
  other arithmetic  1.96 us (1%)
    pallas_call x1, Pallas kernels, reduce_spread(): pl.pallas_call(functools.partial(spread_kernel, n_row, n_col), out_shape=...  102 us
    pallas_call x1, Pallas kernels, gather_window(): pl.pallas_call(functools.partial(gather_kernel, n_row, n_col), out_shape=...  54.2 us
    pallas_call x1, Pallas kernels, local_math(): pl.pallas_call(local_kernel, out_shape=(jax.ShapeDtypeStruct((nodes, widt...  10.1 us

profile of v18, /device:TPU:57, one launch (start us, length us, event | category | flops | bytes accessed | tf_op | source)
XLA Modules:
  0.0 169.9 jit_solution(15379881588991961528)
XLA Ops:
  1.3 54.2 %shard_map.111 = bf16[3,8,256,256]{3,2,1,0:T(8,128)(2,1)} custom-call(bf16[256,256]{1,0:T(8,128)(2,1)} %feat_ref.1), custom_call_target="tpu_custom_call" | custom-call | tf_op jit(solution)/shard_map/pallas_call | solution.py:217
  55.5 10.1 %shard_map.112 = (bf16[256,256]{1,0:T(8,128)(2,1)}, f32[512,256]{1,0:T(8,128)}, f32[256,256]{1,0:T(8,128)}, f32[48,128,256]{2,1,0:T(8,128)}) custom-call(s32[32]{0:T(128)} %bitcast.10, s32[32]{0:T(128)} %bitcast.11, s32[1]{0:T(128)} %bitcast.6.count_ref, bf16[48,128,256]{2,1,0:T(8,128)(2,1)} %bitcast.7, bf16[32,128,128]{2,1,0:T(8,128)(2,1)} %bitcast.9, ...), custom_call_target="tpu_custom_call" | custom-call | tf_op jit(solution)/shard_map/pallas_call | solution.py:491
  65.6 0.0 copy-start
  65.6 102.3 %shard_map.113 = (f32[256,256]{1,0:T(8,128)}, f32[512,256]{1,0:T(8,128)}) custom-call(f32[3,8,256,256]{3,2,1,0:T(8,128)} %bitcast.8, f32[512,256]{1,0:T(8,128)} %get-tuple-element.12.parts_ref), custom_call_target="tpu_custom_call" | custom-call | tf_op jit(solution)/shard_map/pallas_call | solution.py:393
  168.0 0.0 copy-done
  168.0 2.0 %slice_multiply_fusion = (f32[256,256]{1,0:T(8,128)}, f32[256,256]{1,0:T(8,128)}, bf16[256,256]{1,0:T(8,128)(2,1)}) fusion(f32[512,256]{1,0:T(8,128)} %get-tuple-element.15, f32[256,256]{1,0:T(8,128)} %get-tuple-element.13, f32[256,256]{1,0:T(8,128)S(1)} %copy-done), kind=kLoop, calls=%fused_computation | loop fusion | flops 262144 | bytes 1703936 | tf_op jit(solution)/shard_map/mul | solution.py:543
Async XLA Ops:
  65.6 102.3 %copy-start = (f32[256,256]{1,0:T(8,128)S(1)}, f32[256,256]{1,0:T(8,128)}, u32[]{:S(2)}) copy-start(f32[256,256]{1,0:T(8,128)} %get-tuple-element.14) | copy-start | bytes 786436

commit v19 on v18

--- a/solution.py
+++ b/solution.py
@@ -439,14 +439,24 @@
     count = jnp.minimum(count_ref[0], tiles_ref.shape[0])
     acc[...] = jnp.zeros_like(acc)
 
-    def forward(j, carry):
+    last = tiles_ref.shape[0] - 1
+
+    def forward(i, carry):
+        j = 2 * i
+        k = jnp.minimum(j + 1, last)
+        first = jnp.dot(tiles_ref[j], window_ref[cols_ref[j]], preferred_element_type=jnp.float32)
+        second = jnp.dot(tiles_ref[k], window_ref[cols_ref[k]], preferred_element_type=jnp.float32)
         at = pl.multiple_of(rows_ref[j] * tile, tile)
-        acc[pl.ds(at, tile), :] += jnp.dot(
-            tiles_ref[j], window_ref[cols_ref[j]], preferred_element_type=jnp.float32
-        )
+        acc[pl.ds(at, tile), :] += first
+
+        @pl.when(j + 1 < count)
+        def _():
+            at = pl.multiple_of(rows_ref[k] * tile, tile)
+            acc[pl.ds(at, tile), :] += second
+
         return carry
 
-    lax.fori_loop(0, count, forward, 0)
+    lax.fori_loop(0, (count + 1) // 2, forward, 0)
     aggregated = acc[...].astype(jnp.bfloat16)
     features = feat_ref[...]
     pre_act = jnp.dot(aggregated, w_ref[...], preferred_element_type=jnp.float32) + jnp.dot(
@@ -471,15 +481,26 @@
     self_ref[...] = lax.dot_general(grad_pre, ws_ref[...], by_rows, preferred_element_type=jnp.float32)
     spread[...] = jnp.zeros_like(spread)
 
-    def backward(j, carry):
+    def backward(i, carry):
+        j = 2 * i
+        k = jnp.minimum(j + 1, last)
         at = pl.multiple_of(rows_ref[j] * tile, tile)
-        column = cols_ref[j]
-        spread[column] += lax.dot_general(
+        first = lax.dot_general(
             tiles_ref[j], grad_agg[pl.ds(at, tile), :], over_nodes, preferred_element_type=jnp.float32
         )
+        at = pl.multiple_of(rows_ref[k] * tile, tile)
+        second = lax.dot_general(
+            tiles_ref[k], grad_agg[pl.ds(at, tile), :], over_nodes, preferred_element_type=jnp.float32
+        )
+        spread[cols_ref[j]] += first
+
+        @pl.when(j + 1 < count)
+        def _():
+            spread[cols_ref[k]] += second
+
         return carry
 
-    lax.fori_loop(0, count, backward, 0)
+    lax.fori_loop(0, (count + 1) // 2, backward, 0)
 
 
 def local_math(slot_rows, slot_cols, count, window, tiles, features, weight, weight_self, cotangent):

time: 172 us -> 168 us (0.977)
  Pallas kernels: 167 us -> 164 us
    pallas_call x1, Pallas kernels: 10.1 us -> 7.06 us  [local_math(): pl.pallas_call(local_kernel, out_shape=(jax.ShapeDtypeStruct((nodes, widt...]
where the time goes in v19:
time: 168 us; the launch traced here: 167 us
  Pallas kernels  164 us (98%)
  other arithmetic  1.96 us (1%)
    pallas_call x1, Pallas kernels, reduce_spread(): pl.pallas_call(functools.partial(spread_kernel, n_row, n_col), out_shape=...  103 us
    pallas_call x1, Pallas kernels, gather_window(): pl.pallas_call(functools.partial(gather_kernel, n_row, n_col), out_shape=...  54.2 us
    pallas_call x1, Pallas kernels, local_math(): pl.pallas_call(local_kernel, out_shape=(jax.ShapeDtypeStruct((nodes, widt...  7.06 us

profile of v19, /device:TPU:57, one launch (start us, length us, event | category | flops | bytes accessed | tf_op | source)
XLA Modules:
  0.0 167.2 jit_solution(2464717795439042881)
XLA Ops:
  1.3 54.2 %shard_map.111 = bf16[3,8,256,256]{3,2,1,0:T(8,128)(2,1)} custom-call(bf16[256,256]{1,0:T(8,128)(2,1)} %feat_ref.1), custom_call_target="tpu_custom_call" | custom-call | tf_op jit(solution)/shard_map/pallas_call | solution.py:217
  55.5 7.1 %shard_map.112 = (bf16[256,256]{1,0:T(8,128)(2,1)}, f32[512,256]{1,0:T(8,128)}, f32[256,256]{1,0:T(8,128)}, f32[48,128,256]{2,1,0:T(8,128)}) custom-call(s32[32]{0:T(128)} %bitcast.10, s32[32]{0:T(128)} %bitcast.11, s32[1]{0:T(128)} %bitcast.6.count_ref, bf16[48,128,256]{2,1,0:T(8,128)(2,1)} %bitcast.7, bf16[32,128,128]{2,1,0:T(8,128)(2,1)} %bitcast.9, ...), custom_call_target="tpu_custom_call" | custom-call | tf_op jit(solution)/shard_map/pallas_call | solution.py:512
  62.6 0.0 copy-start
  62.6 102.7 %shard_map.113 = (f32[256,256]{1,0:T(8,128)}, f32[512,256]{1,0:T(8,128)}) custom-call(f32[3,8,256,256]{3,2,1,0:T(8,128)} %bitcast.8, f32[512,256]{1,0:T(8,128)} %get-tuple-element.12.parts_ref), custom_call_target="tpu_custom_call" | custom-call | tf_op jit(solution)/shard_map/pallas_call | solution.py:393
  165.2 0.0 copy-done
  165.2 2.0 %slice_multiply_fusion = (f32[256,256]{1,0:T(8,128)}, f32[256,256]{1,0:T(8,128)}, bf16[256,256]{1,0:T(8,128)(2,1)}) fusion(f32[512,256]{1,0:T(8,128)} %get-tuple-element.15, f32[256,256]{1,0:T(8,128)} %get-tuple-element.13, f32[256,256]{1,0:T(8,128)S(1)} %copy-done), kind=kLoop, calls=%fused_computation | loop fusion | flops 262144 | bytes 1703936 | tf_op jit(solution)/shard_map/mul | solution.py:564
Async XLA Ops:
  62.6 102.7 %copy-start = (f32[256,256]{1,0:T(8,128)S(1)}, f32[256,256]{1,0:T(8,128)}, u32[]{:S(2)}) copy-start(f32[256,256]{1,0:T(8,128)} %get-tuple-element.14) | copy-start | bytes 786436

commit v20 on v13

--- a/solution.py
+++ b/solution.py
@@ -355,11 +355,11 @@
         pl.when(far)(finish)
 
     run_together(
-        allreduce_steps(n_row, n_col, row, col, parts_ref, sums_ref, part, gath,
-                        rsend, rrecv, dsend, drecv, gsend, grecv),
         ring_steps(),
         far_steps(0, up_ref, far_up),
         far_steps(1, down_ref, far_down),
+        allreduce_steps(n_row, n_col, row, col, parts_ref, sums_ref, part, gath,
+                        rsend, rrecv, dsend, drecv, gsend, grecv),
     )
     lasts = []
     for side, target, slot, far in ((0, up, 0, far_up), (1, down, 1, far_down)):

time: 174 us -> 178 us (1.023)
  the two profiles are of different devices: /device:TPU:25 before, /device:TPU:9 now
where the time goes in v20:
time: 178 us
  Pallas kernels  173 us (97%)
  local copies, waits for them, and re-layouts  3.42 us (2%)
    pallas_call x1, Pallas kernels, reduce_spread(): pl.pallas_call(functools.partial(spread_kernel, n_row, n_col, scale), out...  107 us
    pallas_call x1, Pallas kernels, gather_window(): pl.pallas_call(functools.partial(gather_kernel, n_row, n_col), out_shape=...  57.7 us
    pallas_call x1, Pallas kernels, local_math(): pl.pallas_call(local_kernel, out_shape=(jax.ShapeDtypeStruct((nodes, widt...  8.72 us

profile of v20, /device:TPU:9, one launch (start us, length us, event | category | flops | bytes accessed | tf_op | source)
XLA Modules:
  0.0 178.1 jit_solution(12909923359736868896)
XLA Ops:
  1.3 57.7 %shard_map.111 = bf16[3,8,256,256]{3,2,1,0:T(8,128)(2,1)} custom-call(bf16[256,256]{1,0:T(8,128)(2,1)} %feat_ref.1), custom_call_target="tpu_custom_call" | custom-call | tf_op jit(solution)/shard_map/pallas_call | solution.py:217
  59.0 8.7 %shard_map.112 = (bf16[256,256]{1,0:T(8,128)(2,1)}, f32[512,256]{1,0:T(8,128)}, f32[256,256]{1,0:T(8,128)}, f32[48,128,256]{2,1,0:T(8,128)}) custom-call(s32[32]{0:T(128)} %bitcast.10, s32[32]{0:T(128)} %bitcast.11, s32[1]{0:T(128)} %bitcast.6.count_ref, bf16[48,128,256]{2,1,0:T(8,128)(2,1)} %bitcast.7, bf16[32,128,128]{2,1,0:T(8,128)(2,1)} %bitcast.9, ...), custom_call_target="tpu_custom_call" | custom-call | tf_op jit(solution)/shard_map/pallas_call | solution.py:492
  67.7 107.0 %shard_map.113 = (bf16[256,256]{1,0:T(8,128)(2,1)}, f32[512,256]{1,0:T(8,128)}) custom-call(f32[3,8,256,256]{3,2,1,0:T(8,128)} %bitcast.8, f32[512,256]{1,0:T(8,128)} %get-tuple-element.12.parts_ref, f32[256,256]{1,0:T(8,128)} %get-tuple-element.13.self_ref), custom_call_target="tpu_custom_call" | custom-call | tf_op jit(solution)/shard_map/pallas_call | solution.py:394
  174.7 1.9 %fusion = (f32[256,256]{1,0:T(8,128)}, f32[256,256]{1,0:T(8,128)}) fusion(f32[512,256]{1,0:T(8,128)} %get-tuple-element.15), kind=kLoop, calls=%fused_computation | loop fusion | bytes 1048576 | tf_op jit(solution)/shard_map/slice | solution.py:544
  176.6 1.6 copy.14

commit v21 on v13

--- a/solution.py
+++ b/solution.py
@@ -309,7 +309,6 @@
 
     def ring_steps():
         for step in range(1, n_col):
-            start_halo(step - 1 + lead)
             value = local_total(step - 1)
             if step > 1:
                 value = value + ring_in[step - 2].astype(jnp.float32)
@@ -323,6 +322,7 @@
                 device_id_type=MESH,
             )
             copy.start()
+            start_halo(step - 1 + lead)
             yield copy
         start_halo(n_col - 1 + lead)
         own[...] = local_total(n_col - 1) + ring_in[n_col - 2].astype(jnp.float32)

time: 174 us -> 173 us (level)
    pallas_call x1, Pallas kernels: 99.3 us -> 106 us  [reduce_spread(): pl.pallas_call(functools.partial(spread_kernel, n_row, n_col, scale), out...]
    pallas_call x1, Pallas kernels: 12.9 us -> 6.96 us  [local_math(): pl.pallas_call(local_kernel, out_shape=(jax.ShapeDtypeStruct((nodes, widt...]
where the time goes in v21:
time: 173 us
  Pallas kernels  169 us (98%)
  local copies, waits for them, and re-layouts  3.42 us (2%)
    pallas_call x1, Pallas kernels, reduce_spread(): pl.pallas_call(functools.partial(spread_kernel, n_row, n_col, scale), out...  106 us
    pallas_call x1, Pallas kernels, gather_window(): pl.pallas_call(functools.partial(gather_kernel, n_row, n_col), out_shape=...  55.6 us
    pallas_call x1, Pallas kernels, local_math(): pl.pallas_call(local_kernel, out_shape=(jax.ShapeDtypeStruct((nodes, widt...  6.96 us

profile of v21, /device:TPU:25, one launch (start us, length us, event | category | flops | bytes accessed | tf_op | source)
XLA Modules:
  0.0 173.3 jit_solution(17123451973322519179)
XLA Ops:
  1.3 55.6 %shard_map.111 = bf16[3,8,256,256]{3,2,1,0:T(8,128)(2,1)} custom-call(bf16[256,256]{1,0:T(8,128)(2,1)} %feat_ref.1), custom_call_target="tpu_custom_call" | custom-call | tf_op jit(solution)/shard_map/pallas_call | solution.py:217
  56.9 7.0 %shard_map.112 = (bf16[256,256]{1,0:T(8,128)(2,1)}, f32[512,256]{1,0:T(8,128)}, f32[256,256]{1,0:T(8,128)}, f32[48,128,256]{2,1,0:T(8,128)}) custom-call(s32[32]{0:T(128)} %bitcast.10, s32[32]{0:T(128)} %bitcast.11, s32[1]{0:T(128)} %bitcast.6.count_ref, bf16[48,128,256]{2,1,0:T(8,128)(2,1)} %bitcast.7, bf16[32,128,128]{2,1,0:T(8,128)(2,1)} %bitcast.9, ...), custom_call_target="tpu_custom_call" | custom-call | tf_op jit(solution)/shard_map/pallas_call | solution.py:492
  63.9 106.0 %shard_map.113 = (bf16[256,256]{1,0:T(8,128)(2,1)}, f32[512,256]{1,0:T(8,128)}) custom-call(f32[3,8,256,256]{3,2,1,0:T(8,128)} %bitcast.8, f32[512,256]{1,0:T(8,128)} %get-tuple-element.12.parts_ref, f32[256,256]{1,0:T(8,128)} %get-tuple-element.13.self_ref), custom_call_target="tpu_custom_call" | custom-call | tf_op jit(solution)/shard_map/pallas_call | solution.py:394
  169.9 1.9 %fusion = (f32[256,256]{1,0:T(8,128)}, f32[256,256]{1,0:T(8,128)}) fusion(f32[512,256]{1,0:T(8,128)} %get-tuple-element.15), kind=kLoop, calls=%fused_computation | loop fusion | bytes 1048576 | tf_op jit(solution)/shard_map/slice | solution.py:544
  171.7 1.6 copy.14
